TPU v7x, 256 devices: a whole 4x4x8 slice. The times are simulated.
256 devices in a mesh: gx: 4 (over y), gy: 8 (over x, core), gz: 8 (over z).
Axes of the slice: x: 4, y: 4, z: 8, core: 2. Of those that a mesh axis runs over, the one named last changes fastest.
Arguments:
- source: float32 [64, 128, 1024], P('gx', 'gy', 'gz'), may hold values from -5 to 5
- conductance: float32 [64, 128, 1024], P('gx', 'gy', 'gz'), may hold values from 0.2 to 2
- pressure_start: float32 [64, 128, 1024], P('gx', 'gy', 'gz'), may hold values from -6 to 6
Outputs:
- pressure: float32 [64, 128, 1024], P('gx', 'gy', 'gz')
- residual: float32 [64, 128, 1024], P('gx', 'gy', 'gz')
All inputs are finite; a program needn't handle non-finite values.
Results may differ from a plain program's by a relative error of at most 0.0003.
Values sent between devices are 32-bit elements; how exact they have to be, the bound alone decides.
A program may use at most 384 MiB of HBM per device.

v0:
```python
import jax
import jax.numpy as jnp
from jax import lax
from jax.sharding import PartitionSpec as P

LEVELS = 3
DEG = 3
COARSE_ITERS = 12


SHIFT = 0.001
UPPER_BOUND = 2.0
SMOOTH_FLOOR = 0.5
COARSE_FLOOR = 0.05


def extended(cells, sides, width):
    for axis, dim in sides:
        count = lax.axis_size(axis)
        head = lax.slice_in_dim(cells, 0, width, axis=dim)
        tail = lax.slice_in_dim(cells, cells.shape[dim] - width, cells.shape[dim], axis=dim)
        cells = jnp.concatenate(
            [
                lax.ppermute(tail, axis, [(i, (i + 1) % count) for i in range(count)]),
                cells,
                lax.ppermute(head, axis, [((i + 1) % count, i) for i in range(count)]),
            ],
            axis=dim,
        )
    return cells


def chebyshev_weights(number, floor_value):
    centre = 0.5 * (UPPER_BOUND + floor_value)
    half_width = 0.5 * (UPPER_BOUND - floor_value)
    ratio = centre / half_width
    factor = 1.0 / ratio
    weights = [(0.0, 1.0 / centre)]
    for _ in range(1, number):
        factor_next = 1.0 / (2.0 * ratio - factor)
        weights.append((factor_next * factor, 2.0 * factor_next / half_width))
        factor = factor_next
    return weights


def operate_global(field, conduct):
    total = SHIFT * field
    for axis_id in range(3):
        for offset in (1, -1):
            face = 0.5 * (conduct + jnp.roll(conduct, -offset, axis_id))
            total = total + face * (field - jnp.roll(field, -offset, axis_id))
    return total


def diagonal_global(conduct):
    total = jnp.full_like(conduct, SHIFT)
    for axis_id in range(3):
        for offset in (1, -1):
            total = total + 0.5 * (conduct + jnp.roll(conduct, -offset, axis_id))
    return total


def smooth_global(field, source, conduct, inverse, weights):
    change = jnp.zeros_like(field)
    for carry, weight in weights:
        resid = source - operate_global(field, conduct)
        change = carry * change + weight * inverse * resid
        field = field + change
    return field


def restrict(field):
    extent_x, extent_y, extent_z = field.shape
    return field.reshape(extent_x // 2, 2, extent_y // 2, 2, extent_z // 2, 2).mean(axis=(1, 3, 5))


def prolong(field):
    extent_x, extent_y, extent_z = field.shape
    spread = jnp.broadcast_to(
        field[:, None, :, None, :, None], (extent_x, 2, extent_y, 2, extent_z, 2)
    )
    return spread.reshape(2 * extent_x, 2 * extent_y, 2 * extent_z)


def coarse_solve(source, conduct):
    inverse = 1.0 / diagonal_global(conduct)
    weights = chebyshev_weights(COARSE_ITERS, COARSE_FLOOR)
    return smooth_global(jnp.zeros_like(source), source, conduct, inverse, weights)


def trimmed(array, margin):
    if margin == 0:
        return array
    return array[
        margin : array.shape[0] - margin,
        margin : array.shape[1] - margin,
        margin : array.shape[2] - margin,
    ]


def shifted(array, axis_id, offset):
    index = [
        slice(1, array.shape[0] - 1),
        slice(1, array.shape[1] - 1),
        slice(1, array.shape[2] - 1),
    ]
    index[axis_id] = slice(1 + offset, array.shape[axis_id] - 1 + offset)
    return array[tuple(index)]


def operate_padded(field, conduct):
    centre = trimmed(field, 1)
    middle = trimmed(conduct, 1)
    total = SHIFT * centre
    for axis_id in range(3):
        for offset in (1, -1):
            face = 0.5 * (middle + shifted(conduct, axis_id, offset))
            total = total + face * (centre - shifted(field, axis_id, offset))
    return total


def diagonal_padded(conduct):
    middle = trimmed(conduct, 1)
    total = jnp.full_like(middle, SHIFT)
    for axis_id in range(3):
        for offset in (1, -1):
            total = total + 0.5 * (middle + shifted(conduct, axis_id, offset))
    return total


def assemble(gathered, block):
    grid_x, grid_y, grid_z = (lax.axis_size("gx"), lax.axis_size("gy"), lax.axis_size("gz"))
    block_x, block_y, block_z = block
    pieces = gathered.reshape(2, grid_x, grid_y, grid_z, block_x, block_y, block_z)
    return pieces.transpose(0, 1, 4, 2, 5, 3, 6).reshape(
        2, grid_x * block_x, grid_y * block_y, grid_z * block_z
    )


def own_block(whole, block):
    block_x, block_y, block_z = block
    corner = (
        lax.axis_index("gx") * block_x,
        lax.axis_index("gy") * block_y,
        lax.axis_index("gz") * block_z,
    )
    return lax.dynamic_slice(whole, corner, block)


def level_cycle(level, source, conduct, start):
    width = 1
    rim_input = conduct[None]
    padded = extended(rim_input, (("gx", 1), ("gy", 2), ("gz", 3)), width)
    conduct_pad = padded[0]
    inverse_pad = 1.0 / diagonal_padded(conduct_pad)
    weights = chebyshev_weights(DEG, SMOOTH_FLOOR)

    def source_at():
        return source

    def smooth_block(field, zero_start):
        change = jnp.zeros_like(field)
        position = 0
        if zero_start:
            change = weights[0][1] * trimmed(inverse_pad, width - 1) * source
            field = change
            position = 1
        while position < len(weights):
            count = min(width, len(weights) - position)
            both = extended(jnp.stack([field, change]), (("gx", 1), ("gy", 2), ("gz", 3)), count)
            field_pad = both[0]
            change_pad = both[1]
            resid = source_at() - operate_padded(field_pad, trimmed(conduct_pad, width - count))
            carry, weight = weights[position]
            change_pad = (
                carry * trimmed(change_pad, 1)
                + weight * trimmed(inverse_pad, width - count) * resid
            )
            field_pad = trimmed(field_pad, 1) + change_pad
            field = field_pad
            change = change_pad
            position = position + count
        return field

    def residual_of(field):
        rim = extended(field, (("gx", 0), ("gy", 1), ("gz", 2)), 1)
        return source - operate_padded(rim, trimmed(conduct_pad, width - 1))

    field = smooth_block(start, level > 0)
    resid = residual_of(field)
    coarse_source = restrict(resid)
    coarse_conduct = 0.25 * restrict(conduct)
    if level + 1 == LEVELS:
        gathered = lax.all_gather(
            jnp.stack([coarse_source, coarse_conduct]), ("gx", "gy", "gz"), axis=1, tiled=True
        )
        whole = assemble(gathered, coarse_source.shape)
        correction = own_block(coarse_solve(whole[0], whole[1]), coarse_source.shape)
    else:
        correction = level_cycle(
            level + 1, coarse_source, coarse_conduct, jnp.zeros_like(coarse_source)
        )
    field = smooth_block(field + prolong(correction), False)
    if level == 0:
        return (field, residual_of(field))
    return field


def per_device(source, conductance, pressure_start):
    pressure, residual = level_cycle(0, source, conductance, pressure_start)
    return (pressure, residual)


def solution(mesh):
    placed = (P("gx", "gy", "gz"), P("gx", "gy", "gz"), P("gx", "gy", "gz"))
    return jax.shard_map(
        per_device,
        mesh=mesh,
        in_specs=placed,
        out_specs=(P("gx", "gy", "gz"), P("gx", "gy", "gz")),
        check_vma=False,
    )
```

profile of v0, /device:TPU:6, one launch (start us, length us, event | category | flops | bytes accessed | tf_op | source)
XLA Modules:
  0.0 515.5 jit_solution(9670224430390955560)
XLA Ops:
  17.1 4.0 collective-permute-start.11
  27.9 8.2 %collective-permute-done.4 = f32[2,18,18,1]{3,2,1,0:T(8,128)S(1)} collective-permute-done((f32[2,18,18,1]{3,2,1,0:T(8,128)S(1)}, f32[2,18,18,1]{3,2,1,0:T(8,128)S(1)}, u32[]{:S(2)}, u32[]{:S(2)}) %collective-permute-start.4) | collective-permute-done | bytes 2624 | tf_op jit(solution)/shard_map/ppermute | solution.py:24
  46.3 3.6 collective-permute-start.17
  49.9 9.8 %reshape.83 = f32[8,2,8,2,64,2]{5,4,3,2,1,0:T(8,128)} reshape(f32[16,16,128]{2,1,0:T(8,128)S(1)} %copy-done.1) | data formatting | bytes 262144 | tf_op jit(solution)/shard_map/reshape | solution.py:74
  59.7 4.0 reduce_sum.54
  64.8 3.3 collective-permute-start.19
  80.3 8.6 %collective-permute-done.22 = f32[2,18,18,1]{3,2,1,0:T(8,128)S(1)} collective-permute-done((f32[2,18,18,1]{3,2,1,0:T(8,128)S(1)}, f32[2,18,18,1]{3,2,1,0:T(8,128)S(1)}, u32[]{:S(2)}, u32[]{:S(2)}) %collective-permute-start.22) | collective-permute-done | bytes 2624 | tf_op jit(solution)/shard_map/ppermute | solution.py:24
  99.9 3.3 collective-permute-start.34
  103.3 5.4 %collective-permute-done.34 = f32[18,18,1]{2,1,0:T(8,128)S(1)} collective-permute-done((f32[18,18,1]{2,1,0:T(8,128)S(1)}, f32[18,18,1]{2,1,0:T(8,128)S(1)}, u32[]{:S(2)}, u32[]{:S(2)}) %collective-permute-start.34) | collective-permute-done | bytes 1328 | tf_op jit(solution)/shard_map/ppermute | solution.py:26
  108.7 3.9 collective-permute-done.35
  112.9 9.8 %reshape.84 = f32[8,2,8,2,64,2]{5,4,3,2,1,0:T(8,128)} reshape(f32[16,16,128]{2,1,0:T(8,128)S(1)} %fusion.68) | data formatting | bytes 262144 | tf_op jit(solution)/shard_map/reshape | solution.py:74
  122.7 4.0 reduce_sum.55
  142.2 3.3 collective-permute-start.43
  152.4 3.7 collective-permute-start.47
  175.4 3.5 collective-permute-done.59
  196.7 3.3 collective-permute-start.67
  206.0 3.7 collective-permute-start.71
  211.8 3.4 collective-permute-start.72
  216.5 3.5 collective-permute-done.73
  223.2 3.4 collective-permute-start.76
  228.2 3.4 collective-permute-done.77
  232.0 72.8 %all_gather.3 = f32[2,512,2,16]{3,2,1,0:T(2,128)S(1)} all-gather(f32[2,2,2,16]{3,2,1,0:T(2,128)S(1)} %pad_maximum_fusion.210), channel_id=1, replica_groups=mesh['gx'=4,'gy'=8,'gz'=8] {'gx','gy','gz'}, dimensions={1}, use_global_device_ids=true | all-gather | bytes 131584 | tf_op jit(solution)/shard_map/all_gather | solution.py:194
  326.9 3.3 collective-permute-start.85
  373.2 3.3 collective-permute-done.100
  411.1 3.9 broadcast_in_dim.36
  415.0 6.9 %reshape.90 = f32[16,16,128]{2,1,0:T(8,128)S(1)} reshape(f32[8,2,8,2,64,2]{5,4,3,2,1,0:T(8,128)} %broadcast_in_dim.36) | data formatting | bytes 262144 | tf_op jit(solution)/shard_map/reshape | solution.py:82
  435.1 7.9 %collective-permute-done.118 = f32[2,18,18,1]{3,2,1,0:T(8,128)S(1)} collective-permute-done((f32[2,18,18,1]{3,2,1,0:T(8,128)S(1)}, f32[2,18,18,1]{3,2,1,0:T(8,128)S(1)}, u32[]{:S(2)}, u32[]{:S(2)}) %collective-permute-start.118) | collective-permute-done | bytes 2624 | tf_op jit(solution)/shard_map/ppermute | solution.py:24
  457.5 8.2 %collective-permute-done.124 = f32[2,18,18,1]{3,2,1,0:T(8,128)S(1)} collective-permute-done((f32[2,18,18,1]{3,2,1,0:T(8,128)S(1)}, f32[2,18,18,1]{3,2,1,0:T(8,128)S(1)}, u32[]{:S(2)}, u32[]{:S(2)}) %collective-permute-start.124) | collective-permute-done | bytes 2624 | tf_op jit(solution)/shard_map/ppermute | solution.py:24
  479.6 9.1 %collective-permute-done.130 = f32[2,18,18,1]{3,2,1,0:T(8,128)S(1)} collective-permute-done((f32[2,18,18,1]{3,2,1,0:T(8,128)S(1)}, f32[2,18,18,1]{3,2,1,0:T(8,128)S(1)}, u32[]{:S(2)}, u32[]{:S(2)}) %collective-permute-start.130) | collective-permute-done | bytes 2624 | tf_op jit(solution)/shard_map/ppermute | solution.py:24
  495.5 3.5 collective-permute-done.133
  504.9 5.8 %collective-permute-done.136 = f32[18,18,1]{2,1,0:T(8,128)S(1)} collective-permute-done((f32[18,18,1]{2,1,0:T(8,128)S(1)}, f32[18,18,1]{2,1,0:T(8,128)S(1)}, u32[]{:S(2)}, u32[]{:S(2)}) %collective-permute-start.136) | collective-permute-done | bytes 1328 | tf_op jit(solution)/shard_map/ppermute | solution.py:26
  510.7 3.4 collective-permute-done.137
  (526 shorter events, 285.4 us)
Async XLA Ops:
  1.4 8.1 %collective-permute-start.6 = (f32[1,1,16,128]{3,2,1,0:T(8,128)S(1)}, f32[1,1,16,128]{3,2,1,0:T(8,128)S(1)}, u32[]{:S(2)}, u32[]{:S(2)}) collective-permute-start(f32[1,1,16,128]{3,2,1,0:T(8,128)S(1)} %get-tuple-element.153), channel_id=1, source_target_pairs={{0,64},{64,128},{128,192},{192,0},{1,65},{65,129},{129,193},{193,1... | collective-permute-start | bytes 24584 | tf_op jit(solution)/shard_map/ppermute | solution.py:24
  5.4 6.8 %collective-permute-start = (f32[2,1,16,128]{3,2,1,0:T(8,128)S(1)}, f32[2,1,16,128]{3,2,1,0:T(8,128)S(1)}, u32[]{:S(2)}, u32[]{:S(2)}) collective-permute-start(f32[2,1,16,128]{3,2,1,0:T(8,128)S(1)} %get-tuple-element.155), channel_id=1, source_target_pairs={{0,64},{64,128},{128,192},{192,0},{1,65},{65,129},{129,193},{193,1... | collective-permute-start | bytes 49160 | tf_op jit(solution)/shard_map/ppermute | solution.py:24
  12.2 8.9 %collective-permute-start.2 = (f32[2,18,1,128]{3,2,1,0:T(1,128)S(1)}, f32[2,18,1,128]{3,2,1,0:T(1,128)S(1)}, u32[]{:S(2)}, u32[]{:S(2)}) collective-permute-start(f32[2,18,1,128]{3,2,1,0:T(1,128)S(1)} %get-tuple-element.105), channel_id=1, source_target_pairs={{0,8},{8,16},{16,24},{24,32},{32,40},{40,48},{48,56},{56,0},{1,9},... | collective-permute-start | bytes 55304 | tf_op jit(solution)/shard_map/ppermute | solution.py:24
  12.9 8.3 %collective-permute-start.3 = (f32[2,18,1,128]{3,2,1,0:T(1,128)S(1)}, f32[2,18,1,128]{3,2,1,0:T(1,128)S(1)}, u32[]{:S(2)}, u32[]{:S(2)}) collective-permute-start(f32[2,18,1,128]{3,2,1,0:T(1,128)S(1)} %get-tuple-element.106), channel_id=1, source_target_pairs={{8,0},{16,8},{24,16},{32,24},{40,32},{48,40},{56,48},{0,56},{9,1},... | collective-permute-start | bytes 55304 | tf_op jit(solution)/shard_map/ppermute | solution.py:26
  15.1 11.6 %collective-permute-start.10 = (f32[1,18,18,1]{3,2,1,0:T(8,128)S(1)}, f32[1,18,18,1]{3,2,1,0:T(8,128)S(1)}, u32[]{:S(2)}, u32[]{:S(2)}) collective-permute-start(f32[1,18,18,1]{3,2,1,0:T(8,128)S(1)} %get-tuple-element.119), channel_id=1, source_target_pairs={{0,1},{1,2},{2,3},{3,4},{4,5},{5,6},{6,7},{7,0},{8,9},{9,10},{10,1... | collective-permute-start | bytes 3896 | tf_op jit(solution)/shard_map/ppermute | solution.py:24
  17.1 9.6 %collective-permute-start.11 = (f32[1,18,18,1]{3,2,1,0:T(8,128)S(1)}, f32[1,18,18,1]{3,2,1,0:T(8,128)S(1)}, u32[]{:S(2)}, u32[]{:S(2)}) collective-permute-start(f32[1,18,18,1]{3,2,1,0:T(8,128)S(1)} %get-tuple-element.120), channel_id=1, source_target_pairs={{1,0},{2,1},{3,2},{4,3},{5,4},{6,5},{7,6},{0,7},{9,8},{10,9},{11,1... | collective-permute-start | bytes 3896 | tf_op jit(solution)/shard_map/ppermute | solution.py:26
  21.4 14.8 %collective-permute-start.4 = (f32[2,18,18,1]{3,2,1,0:T(8,128)S(1)}, f32[2,18,18,1]{3,2,1,0:T(8,128)S(1)}, u32[]{:S(2)}, u32[]{:S(2)}) collective-permute-start(f32[2,18,18,1]{3,2,1,0:T(8,128)S(1)} %get-tuple-element.93), channel_id=1, source_target_pairs={{0,1},{1,2},{2,3},{3,4},{4,5},{5,6},{6,7},{7,0},{8,9},{9,10},{10,1... | collective-permute-start | bytes 7784 | tf_op jit(solution)/shard_map/ppermute | solution.py:24
  21.5 14.7 %collective-permute-start.5 = (f32[2,18,18,1]{3,2,1,0:T(8,128)S(1)}, f32[2,18,18,1]{3,2,1,0:T(8,128)S(1)}, u32[]{:S(2)}, u32[]{:S(2)}) collective-permute-start(f32[2,18,18,1]{3,2,1,0:T(8,128)S(1)} %get-tuple-element.94), channel_id=1, source_target_pairs={{1,0},{2,1},{3,2},{4,3},{5,4},{6,5},{7,6},{0,7},{9,8},{10,9},{11,1... | collective-permute-start | bytes 7784 | tf_op jit(solution)/shard_map/ppermute | solution.py:26
  45.9 17.8 %collective-permute-start.16 = (f32[2,18,18,1]{3,2,1,0:T(8,128)S(1)}, f32[2,18,18,1]{3,2,1,0:T(8,128)S(1)}, u32[]{:S(2)}, u32[]{:S(2)}) collective-permute-start(f32[2,18,18,1]{3,2,1,0:T(8,128)S(1)} %get-tuple-element.91), channel_id=1, source_target_pairs={{0,1},{1,2},{2,3},{3,4},{4,5},{5,6},{6,7},{7,0},{8,9},{9,10},{10,1... | collective-permute-start | bytes 7784 | tf_op jit(solution)/shard_map/ppermute | solution.py:24
  46.3 17.4 %collective-permute-start.17 = (f32[2,18,18,1]{3,2,1,0:T(8,128)S(1)}, f32[2,18,18,1]{3,2,1,0:T(8,128)S(1)}, u32[]{:S(2)}, u32[]{:S(2)}) collective-permute-start(f32[2,18,18,1]{3,2,1,0:T(8,128)S(1)} %get-tuple-element.92), channel_id=1, source_target_pairs={{1,0},{2,1},{3,2},{4,3},{5,4},{6,5},{7,6},{0,7},{9,8},{10,9},{11,1... | collective-permute-start | bytes 7784 | tf_op jit(solution)/shard_map/ppermute | solution.py:26
  71.6 6.9 %collective-permute-start.24 = (f32[1,1,8,64]{3,2,1,0:T(8,128)S(1)}, f32[1,1,8,64]{3,2,1,0:T(8,128)S(1)}, u32[]{:S(2)}, u32[]{:S(2)}) collective-permute-start(f32[1,1,8,64]{3,2,1,0:T(8,128)S(1)} %get-tuple-element.356), channel_id=1, source_target_pairs={{0,64},{64,128},{128,192},{192,0},{1,65},{65,129},{129,193},{193,1... | collective-permute-start | bytes 6152 | tf_op jit(solution)/shard_map/ppermute | solution.py:24
  75.2 13.7 %collective-permute-start.22 = (f32[2,18,18,1]{3,2,1,0:T(8,128)S(1)}, f32[2,18,18,1]{3,2,1,0:T(8,128)S(1)}, u32[]{:S(2)}, u32[]{:S(2)}) collective-permute-start(f32[2,18,18,1]{3,2,1,0:T(8,128)S(1)} %get-tuple-element.89), channel_id=1, source_target_pairs={{0,1},{1,2},{2,3},{3,4},{4,5},{5,6},{6,7},{7,0},{8,9},{9,10},{10,1... | collective-permute-start | bytes 7784 | tf_op jit(solution)/shard_map/ppermute | solution.py:24
  75.3 13.8 %collective-permute-start.23 = (f32[2,18,18,1]{3,2,1,0:T(8,128)S(1)}, f32[2,18,18,1]{3,2,1,0:T(8,128)S(1)}, u32[]{:S(2)}, u32[]{:S(2)}) collective-permute-start(f32[2,18,18,1]{3,2,1,0:T(8,128)S(1)} %get-tuple-element.90), channel_id=1, source_target_pairs={{1,0},{2,1},{3,2},{4,3},{5,4},{6,5},{7,6},{0,7},{9,8},{10,9},{11,1... | collective-permute-start | bytes 7784 | tf_op jit(solution)/shard_map/ppermute | solution.py:26
  78.5 13.6 %collective-permute-start.26 = (f32[1,10,1,64]{3,2,1,0:T(1,128)S(1)}, f32[1,10,1,64]{3,2,1,0:T(1,128)S(1)}, u32[]{:S(2)}, u32[]{:S(2)}) collective-permute-start(f32[1,10,1,64]{3,2,1,0:T(1,128)S(1)} %get-tuple-element.346), channel_id=1, source_target_pairs={{0,8},{8,16},{16,24},{24,32},{32,40},{40,48},{48,56},{56,0},{1,9},... | collective-permute-start | bytes 7688 | tf_op jit(solution)/shard_map/ppermute | solution.py:24
  79.6 12.5 %collective-permute-start.27 = (f32[1,10,1,64]{3,2,1,0:T(1,128)S(1)}, f32[1,10,1,64]{3,2,1,0:T(1,128)S(1)}, u32[]{:S(2)}, u32[]{:S(2)}) collective-permute-start(f32[1,10,1,64]{3,2,1,0:T(1,128)S(1)} %get-tuple-element.347), channel_id=1, source_target_pairs={{8,0},{16,8},{24,16},{32,24},{40,32},{48,40},{56,48},{0,56},{9,1},... | collective-permute-start | bytes 7688 | tf_op jit(solution)/shard_map/ppermute | solution.py:26
  96.2 6.9 %collective-permute-start.28 = (f32[1,10,10,1]{3,2,1,0:T(8,128)S(1)}, f32[1,10,10,1]{3,2,1,0:T(8,128)S(1)}, u32[]{:S(2)}, u32[]{:S(2)}) collective-permute-start(f32[1,10,10,1]{3,2,1,0:T(8,128)S(1)} %get-tuple-element.167), channel_id=1, source_target_pairs={{0,1},{1,2},{2,3},{3,4},{4,5},{5,6},{6,7},{7,0},{8,9},{9,10},{10,1... | collective-permute-start | bytes 1208 | tf_op jit(solution)/shard_map/ppermute | solution.py:24
  99.9 8.9 %collective-permute-start.34 = (f32[18,18,1]{2,1,0:T(8,128)S(1)}, f32[18,18,1]{2,1,0:T(8,128)S(1)}, u32[]{:S(2)}, u32[]{:S(2)}) collective-permute-start(f32[18,18,1]{2,1,0:T(8,128)S(1)} %get-tuple-element.117), channel_id=1, source_target_pairs={{1,0},{2,1},{3,2},{4,3},{5,4},{6,5},{7,6},{0,7},{9,8},{10,9},{11,1... | collective-permute-start | bytes 3896 | tf_op jit(solution)/shard_map/ppermute | solution.py:26
  103.2 9.5 %collective-permute-start.35 = (f32[18,18,1]{2,1,0:T(8,128)S(1)}, f32[18,18,1]{2,1,0:T(8,128)S(1)}, u32[]{:S(2)}, u32[]{:S(2)}) collective-permute-start(f32[18,18,1]{2,1,0:T(8,128)S(1)} %get-tuple-element.118), channel_id=1, source_target_pairs={{0,1},{1,2},{2,3},{3,4},{4,5},{5,6},{6,7},{7,0},{8,9},{9,10},{10,1... | collective-permute-start | bytes 3896 | tf_op jit(solution)/shard_map/ppermute | solution.py:24
  135.1 6.6 %collective-permute-start.40 = (f32[2,10,10,1]{3,2,1,0:T(8,128)S(1)}, f32[2,10,10,1]{3,2,1,0:T(8,128)S(1)}, u32[]{:S(2)}, u32[]{:S(2)}) collective-permute-start(f32[2,10,10,1]{3,2,1,0:T(8,128)S(1)} %get-tuple-element.139), channel_id=1, source_target_pairs={{0,1},{1,2},{2,3},{3,4},{4,5},{5,6},{6,7},{7,0},{8,9},{9,10},{10,1... | collective-permute-start | bytes 2408 | tf_op jit(solution)/shard_map/ppermute | solution.py:24
  148.8 7.3 %collective-permute-start.48 = (f32[1,1,4,32]{3,2,1,0:T(4,128)S(1)}, f32[1,1,4,32]{3,2,1,0:T(4,128)S(1)}, u32[]{:S(2)}, u32[]{:S(2)}) collective-permute-start(f32[1,1,4,32]{3,2,1,0:T(4,128)S(1)} %get-tuple-element.390), channel_id=1, source_target_pairs={{0,64},{64,128},{128,192},{192,0},{1,65},{65,129},{129,193},{193,1... | collective-permute-start | bytes 1544 | tf_op jit(solution)/shard_map/ppermute | solution.py:24
  152.3 7.5 %collective-permute-start.46 = (f32[2,10,10,1]{3,2,1,0:T(8,128)S(1)}, f32[2,10,10,1]{3,2,1,0:T(8,128)S(1)}, u32[]{:S(2)}, u32[]{:S(2)}) collective-permute-start(f32[2,10,10,1]{3,2,1,0:T(8,128)S(1)} %get-tuple-element.135), channel_id=1, source_target_pairs={{0,1},{1,2},{2,3},{3,4},{4,5},{5,6},{6,7},{7,0},{8,9},{9,10},{10,1... | collective-permute-start | bytes 2408 | tf_op jit(solution)/shard_map/ppermute | solution.py:24
  152.4 7.5 %collective-permute-start.47 = (f32[2,10,10,1]{3,2,1,0:T(8,128)S(1)}, f32[2,10,10,1]{3,2,1,0:T(8,128)S(1)}, u32[]{:S(2)}, u32[]{:S(2)}) collective-permute-start(f32[2,10,10,1]{3,2,1,0:T(8,128)S(1)} %get-tuple-element.136), channel_id=1, source_target_pairs={{1,0},{2,1},{3,2},{4,3},{5,4},{6,5},{7,6},{0,7},{9,8},{10,9},{11,1... | collective-permute-start | bytes 2408 | tf_op jit(solution)/shard_map/ppermute | solution.py:26
  369.9 6.6 %collective-permute-start.100 = (f32[2,10,10,1]{3,2,1,0:T(8,128)S(1)}, f32[2,10,10,1]{3,2,1,0:T(8,128)S(1)}, u32[]{:S(2)}, u32[]{:S(2)}) collective-permute-start(f32[2,10,10,1]{3,2,1,0:T(8,128)S(1)} %get-tuple-element.131), channel_id=1, source_target_pairs={{0,1},{1,2},{2,3},{3,4},{4,5},{5,6},{6,7},{7,0},{8,9},{9,10},{10,1... | collective-permute-start | bytes 2408 | tf_op jit(solution)/shard_map/ppermute | solution.py:24
  387.2 6.6 %collective-permute-start.106 = (f32[2,10,10,1]{3,2,1,0:T(8,128)S(1)}, f32[2,10,10,1]{3,2,1,0:T(8,128)S(1)}, u32[]{:S(2)}, u32[]{:S(2)}) collective-permute-start(f32[2,10,10,1]{3,2,1,0:T(8,128)S(1)} %get-tuple-element.127), channel_id=1, source_target_pairs={{0,1},{1,2},{2,3},{3,4},{4,5},{5,6},{6,7},{7,0},{8,9},{9,10},{10,1... | collective-permute-start | bytes 2408 | tf_op jit(solution)/shard_map/ppermute | solution.py:24
  431.7 11.3 %collective-permute-start.118 = (f32[2,18,18,1]{3,2,1,0:T(8,128)S(1)}, f32[2,18,18,1]{3,2,1,0:T(8,128)S(1)}, u32[]{:S(2)}, u32[]{:S(2)}) collective-permute-start(f32[2,18,18,1]{3,2,1,0:T(8,128)S(1)} %get-tuple-element.87), channel_id=1, source_target_pairs={{0,1},{1,2},{2,3},{3,4},{4,5},{5,6},{6,7},{7,0},{8,9},{9,10},{10,1... | collective-permute-start | bytes 7784 | tf_op jit(solution)/shard_map/ppermute | solution.py:24
  433.1 10.5 %collective-permute-start.119 = (f32[2,18,18,1]{3,2,1,0:T(8,128)S(1)}, f32[2,18,18,1]{3,2,1,0:T(8,128)S(1)}, u32[]{:S(2)}, u32[]{:S(2)}) collective-permute-start(f32[2,18,18,1]{3,2,1,0:T(8,128)S(1)} %get-tuple-element.88), channel_id=1, source_target_pairs={{1,0},{2,1},{3,2},{4,3},{5,4},{6,5},{7,6},{0,7},{9,8},{10,9},{11,1... | collective-permute-start | bytes 7784 | tf_op jit(solution)/shard_map/ppermute | solution.py:26
  453.9 11.8 %collective-permute-start.124 = (f32[2,18,18,1]{3,2,1,0:T(8,128)S(1)}, f32[2,18,18,1]{3,2,1,0:T(8,128)S(1)}, u32[]{:S(2)}, u32[]{:S(2)}) collective-permute-start(f32[2,18,18,1]{3,2,1,0:T(8,128)S(1)} %get-tuple-element.85), channel_id=1, source_target_pairs={{0,1},{1,2},{2,3},{3,4},{4,5},{5,6},{6,7},{7,0},{8,9},{9,10},{10,1... | collective-permute-start | bytes 7784 | tf_op jit(solution)/shard_map/ppermute | solution.py:24
  455.5 11.1 %collective-permute-start.125 = (f32[2,18,18,1]{3,2,1,0:T(8,128)S(1)}, f32[2,18,18,1]{3,2,1,0:T(8,128)S(1)}, u32[]{:S(2)}, u32[]{:S(2)}) collective-permute-start(f32[2,18,18,1]{3,2,1,0:T(8,128)S(1)} %get-tuple-element.86), channel_id=1, source_target_pairs={{1,0},{2,1},{3,2},{4,3},{5,4},{6,5},{7,6},{0,7},{9,8},{10,9},{11,1... | collective-permute-start | bytes 7784 | tf_op jit(solution)/shard_map/ppermute | solution.py:26
  476.3 12.4 %collective-permute-start.130 = (f32[2,18,18,1]{3,2,1,0:T(8,128)S(1)}, f32[2,18,18,1]{3,2,1,0:T(8,128)S(1)}, u32[]{:S(2)}, u32[]{:S(2)}) collective-permute-start(f32[2,18,18,1]{3,2,1,0:T(8,128)S(1)} %get-tuple-element.83), channel_id=1, source_target_pairs={{0,1},{1,2},{2,3},{3,4},{4,5},{5,6},{6,7},{7,0},{8,9},{9,10},{10,1... | collective-permute-start | bytes 7784 | tf_op jit(solution)/shard_map/ppermute | solution.py:24
  477.6 12.2 %collective-permute-start.131 = (f32[2,18,18,1]{3,2,1,0:T(8,128)S(1)}, f32[2,18,18,1]{3,2,1,0:T(8,128)S(1)}, u32[]{:S(2)}, u32[]{:S(2)}) collective-permute-start(f32[2,18,18,1]{3,2,1,0:T(8,128)S(1)} %get-tuple-element.84), channel_id=1, source_target_pairs={{1,0},{2,1},{3,2},{4,3},{5,4},{6,5},{7,6},{0,7},{9,8},{10,9},{11,1... | collective-permute-start | bytes 7784 | tf_op jit(solution)/shard_map/ppermute | solution.py:26
  502.3 8.5 %collective-permute-start.136 = (f32[18,18,1]{2,1,0:T(8,128)S(1)}, f32[18,18,1]{2,1,0:T(8,128)S(1)}, u32[]{:S(2)}, u32[]{:S(2)}) collective-permute-start(f32[18,18,1]{2,1,0:T(8,128)S(1)} %get-tuple-element.115), channel_id=1, source_target_pairs={{1,0},{2,1},{3,2},{4,3},{5,4},{6,5},{7,6},{0,7},{9,8},{10,9},{11,1... | collective-permute-start | bytes 3896 | tf_op jit(solution)/shard_map/ppermute | solution.py:26
  504.9 9.2 %collective-permute-start.137 = (f32[18,18,1]{2,1,0:T(8,128)S(1)}, f32[18,18,1]{2,1,0:T(8,128)S(1)}, u32[]{:S(2)}, u32[]{:S(2)}) collective-permute-start(f32[18,18,1]{2,1,0:T(8,128)S(1)} %get-tuple-element.116), channel_id=1, source_target_pairs={{0,1},{1,2},{2,3},{3,4},{4,5},{5,6},{6,7},{7,0},{8,9},{9,10},{10,1... | collective-permute-start | bytes 3896 | tf_op jit(solution)/shard_map/ppermute | solution.py:24
  (109 other events, 569.0 us)
where the time goes:
time: 524 us; the launch traced here: 515 us
  starting transfers between devices  191 us (36%)
  waiting for transfers between devices  182 us (35%)
  blocking collectives  72.8 us (14%)
  local copies, waits for them, and re-layouts  42.4 us (8%)
  other arithmetic  25.1 us (5%)
    ppermute x69, waiting for transfers between devices, extended(): lax.ppermute(tail, axis, [(i, (i + 1) % count) for i in range(count)])  137 us
    ppermute x69, starting transfers between devices, extended(): lax.ppermute(head, axis, [((i + 1) % count, i) for i in range(count)])  130 us
    all_gather x1, blocking collectives, level_cycle(): lax.all_gather(jnp.stack([coarse_source, coarse_conduct]), ('gx', 'gy', '...  72.8 us
    ppermute x69, starting transfers between devices, extended(): lax.ppermute(tail, axis, [(i, (i + 1) % count) for i in range(count)])  60.4 us
    ppermute x69, waiting for transfers between devices, extended(): lax.ppermute(head, axis, [((i + 1) % count, i) for i in range(count)])  44.6 us
    reshape x4, local copies, waits for them, and re-layouts, restrict(): field.reshape(extent_x // 2, 2, extent_y // 2, 2, extent_z // 2, 2)  20.8 us
  transfers between devices with their start and end apart: 138, of which 92 were waited for; matrix products, arithmetic and copies ran while one was open for 4% of the time, Pallas kernels for 0%

commit v1 on v0

v1 whole, which is shorter than its diff:
```python
import functools
import jax
import jax.numpy as jnp
from jax import lax
from jax.experimental import pallas as pl
from jax.experimental.pallas import tpu as pltpu
from jax.sharding import PartitionSpec as P

DEG = 3
COARSE_ITERS = 12
SHIFT = 0.001
UPPER_BOUND = 2.0
SMOOTH_FLOOR = 0.5
COARSE_FLOOR = 0.05

MESH = pl.DeviceIdType.MESH
AXES = ("gx", "gy", "gz")
COUNT = (4, 8, 8)
F32 = jnp.float32
SIGN = (1, -1)

NEAR = [
    (a, b, c)
    for c in (-1, 0, 1)
    for a in (-1, 0, 1)
    for b in (-1, 0, 1)
    if (a, b, c) != (0, 0, 0)
]
NEAR.sort(key=lambda o: -sum(map(abs, o)))
PLANE = [(a, b, 0) for a in range(4) for b in range(8) if (a, b) != (0, 0)]
RING = [(0, 0, c) for c in range(1, 8)]


def chebyshev_weights(number, floor_value):
    centre = 0.5 * (UPPER_BOUND + floor_value)
    half_width = 0.5 * (UPPER_BOUND - floor_value)
    ratio = centre / half_width
    factor = 1.0 / ratio
    weights = [(0.0, 1.0 / centre)]
    for _ in range(1, number):
        factor_next = 1.0 / (2.0 * ratio - factor)
        weights.append((factor_next * factor, 2.0 * factor_next / half_width))
        factor = factor_next
    return weights


def peer(offset):
    return tuple(
        lax.rem(lax.axis_index(axis) + (step + count), count)
        for axis, step, count in zip(AXES, offset, COUNT)
    )


def iota(shape, dim):
    return lax.broadcasted_iota(jnp.int32, shape, dim)


def roll(value, shift, dim):
    size = value.shape[dim]
    return pltpu.roll(value, shift % size, dim)


def dot(left, right):
    return jnp.dot(left, right, precision=lax.Precision.HIGHEST, preferred_element_type=F32)


def ones_where(mask, scale=1.0):
    return jnp.where(mask, F32(scale), F32(0.0))


def send(src, dst, ssem, rsem, offset):
    pltpu.make_async_remote_copy(
        src_ref=src, dst_ref=dst, send_sem=ssem, recv_sem=rsem,
        device_id=peer(offset), device_id_type=MESH,
    ).start()


def wait_bytes(ref, sem):
    pltpu.make_async_copy(ref, ref, sem).wait()


def pack_fine(ext, count, py, pz):
    sub = iota((8, 128), 0)
    lane = iota((8, 128), 1)
    for a in range(count):
        for group in range(4):
            for r in range(2):
                first = 4 + 4 * group + r
                slot = 2 * group + r
                py[0, a, slot] = jnp.where(
                    sub >= 4, ext[a, first, 8:16, 0:128], roll(ext[a, first + 2, 8:16, 0:128], 4, 0)
                )
                py[1, a, slot] = jnp.where(
                    sub < 4, ext[a, first, 0:8, 0:128], roll(ext[a, first + 2, 0:8, 0:128], 4, 0)
                )
        for tile in range(2):
            acc = jnp.zeros((8, 128), F32)
            for x in range(16):
                row = ext[a, 4 + x, 8 * tile : 8 * tile + 8, 0:128]
                acc = jnp.where(lane // 8 == x, roll(row, 8 * x + 4, 1), acc)
            pz[a, tile] = acc


def send_fine(ext, py, pz, recv, ssem, rsem):
    ry, rz, rxy, rxz, ryz, rxyz = recv
    for offset in NEAR:
        dx, dy, dz = offset
        xi, yi, zi = (0 if d == 1 else 1 for d in offset)
        kind = (dx != 0, dy != 0, dz != 0)
        tile = 1 if dy == 1 else 0
        planes = pl.ds(6, 2) if dx == 1 else pl.ds(0, 2)
        if kind == (True, False, False):
            src = ext.at[:, pl.ds(16 if dx == 1 else 4, 4), pl.ds(0, 16), pl.ds(0, 128)]
            dst = ext.at[:, pl.ds(0 if dx == 1 else 20, 4), pl.ds(0, 16), pl.ds(0, 128)]
            which = 0
        elif kind == (False, True, False):
            src, dst, which = py.at[yi], ry.at[yi], 1
        elif kind == (False, False, True):
            src, dst, which = pz, rz.at[zi], 2
        elif kind == (True, True, False):
            src, dst, which = py.at[yi, :, planes], rxy.at[xi, yi], 3
        elif kind == (True, False, True):
            src, dst, which = pz, rxz.at[xi, zi], 4
        elif kind == (False, True, True):
            src, dst, which = pz.at[:, tile], ryz.at[yi, zi], 5
        else:
            src, dst, which = pz.at[:, tile], rxyz.at[xi, yi, zi], 6
        send(src, dst, ssem.at[which], rsem.at[which], offset)


def wait_fine(py, recv, sem):
    refs = (recv[0].at[:, :, pl.ds(0, 8)],) + recv
    for which in range(7):
        wait_bytes(refs[which], sem.at[which])


def unpack_fine(ext, count, recv):
    ry, rz, rxy, rxz, ryz, rxyz = recv
    sub = iota((8, 128), 0)
    lane = iota((8, 128), 1)
    low = sub < 4
    zleft = lane % 8 < 4

    def place(a, first, left, right):
        ext[a, first, 16:24, 0:128] = jnp.where(low, right, left)
        ext[a, first + 2, 16:24, 0:128] = roll(jnp.where(low, left, right), 4, 0)

    for a in range(count):
        for group in range(4):
            for r in range(2):
                slot = 2 * group + r
                place(a, 4 + 4 * group + r, ry[0, a, slot], ry[1, a, slot])
        for r in range(2):
            place(a, r, rxy[0, 0, a, r], rxy[0, 1, a, r])
            place(a, 20 + r, rxy[1, 0, a, r], rxy[1, 1, a, r])
        for part in range(3):
            for tile in range(3):
                both = []
                for zi in range(2):
                    if tile < 2:
                        both.append(rz[zi, a, tile] if part == 0 else rxz[part - 1, zi, a, tile])
                    elif part == 0:
                        both.append(jnp.where(low, ryz[1, zi, a], ryz[0, zi, a]))
                    else:
                        both.append(jnp.where(low, rxyz[part - 1, 1, zi, a], rxyz[part - 1, 0, zi, a]))
                comb = jnp.where(zleft, both[0], both[1])
                if part == 0:
                    pairs = [(4 + x, x) for x in range(16)]
                elif part == 1:
                    pairs = [(j, 12 + j) for j in range(4)]
                else:
                    pairs = [(20 + j, j) for j in range(4)]
                for plane, x in pairs:
                    ext[a, plane, 8 * tile : 8 * tile + 8, 128:256] = roll(comb, -(8 * x + 4), 1)


def planes_loop(first, last, unroll, body):
    total = last - first
    while total % unroll:
        unroll -= 1

    def step(i, carry):
        for u in range(unroll):
            body(first + i * unroll + u)
        return carry

    lax.fori_loop(0, total // unroll, step, 0)


def make_coefficients(load, coef, diag, inverse, x):
    k = load(x)
    faces = [0.5 * (k + load(x + 1)), 0.5 * (k + load(x - 1))]
    yp = 0.5 * (k + roll(k, -1, 0))
    zp = 0.5 * (k + roll(k, -1, 1))
    faces += [yp, roll(yp, 1, 0), zp, roll(zp, 1, 1)]
    d = SHIFT + ((faces[0] + faces[1]) + (faces[2] + faces[3]) + (faces[4] + faces[5]))
    inv = 1.0 / d
    for n in range(6):
        coef[n, x] = faces[n] * inv
    diag[x] = d
    inverse[x] = inv
    return inv


def scaled_residual(load, coef, scaled, x):
    v = load(x)
    total = scaled[x] - v
    total = total + (coef[0, x] * load(x + 1) + coef[1, x] * load(x - 1))
    total = total + (coef[2, x] * roll(v, -1, 0) + coef[3, x] * roll(v, 1, 0))
    total = total + (coef[4, x] * roll(v, -1, 1) + coef[5, x] * roll(v, 1, 1))
    return v, total


def shifts_plane(ref, ix):
    sub = iota((8, 8, 128), 1)
    lane = iota((8, 8, 128), 2)
    cur = ref[ix]
    nxt = jnp.concatenate([cur[1:], cur[:1]], axis=0)
    prv = jnp.concatenate([cur[7:], cur[:7]], axis=0)
    yp = jnp.where(sub % 4 == 3, roll(nxt, 3, 1), roll(cur, -1, 1))
    ym = jnp.where(sub % 4 == 0, roll(prv, -3, 1), roll(cur, 1, 1))
    half = roll(cur, 4, 1)
    swap = roll(half, 64, 2)
    swap_next = roll(roll(ref[(ix + 1) % 4], 4, 1), 64, 2)
    swap_prev = roll(roll(ref[(ix + 3) % 4], 4, 1), 64, 2)
    xp = jnp.where(sub < 4, half, jnp.where(lane < 64, swap, swap_next))
    xm = jnp.where(sub >= 4, half, jnp.where(lane >= 64, swap, swap_prev))
    return cur, (xp, xm, yp, ym, roll(cur, -1, 2), roll(cur, 1, 2))


def kernel(
    source, conductance, start, pressure, residual,
    ea, ev, va, vb, w0, fi0, coef0, diag0, inv0, py, pz, pyv, pzv,
    ry, rz, rxy, rxz, ryz, rxyz, ryv, rzv, rxyv, rxzv, ryzv, rxyzv,
    tk, tf, k1, v1a, v1b, w1, fi1, coef1, diag1, inv1,
    gk, gf, mk, mf, v2a, v2b, w2, coef2, diag2, inv2,
    ck, cf, k3, f3, v3a, v3b, w3, coef3,
    sem_s, sem_r, semv_s, semv_r, sem1,
):
    weights = chebyshev_weights(DEG, SMOOTH_FLOOR)
    coarse_weights = chebyshev_weights(COARSE_ITERS, COARSE_FLOOR)
    gx, gy, gz = (lax.axis_index(axis) for axis in AXES)
    recv = (ry, rz, rxy, rxz, ryz, rxyz)
    recv_v = (ryv, rzv, rxyv, rxzv, ryzv, rxyzv)

    everyone = list(dict.fromkeys(
        [tuple(s % n for s, n in zip(o, COUNT)) for o in NEAR + PLANE + RING]
    ))
    barrier = pltpu.get_barrier_semaphore()
    for offset in everyone:
        pl.semaphore_signal(barrier, inc=1, device_id=peer(offset), device_id_type=MESH)

    for a, ref in enumerate((start, conductance, source)):
        ea[a, 4:20, 0:16, 0:128] = ref[...]
    pack_fine(ea, 3, py, pz)
    pl.semaphore_wait(barrier, len(everyone))
    send_fine(ea, py, pz, recv, sem_s, sem_r)

    def restrict_fine(load, scale):
        rows = [
            jnp.concatenate([load(2 * p) + load(2 * p + 1), load(2 * p + 8) + load(2 * p + 9)], axis=1)
            for p in range(4)
        ]
        i, j = iota((256, 128), 0), iota((256, 128), 1)
        right = ones_where((i // 128 == j // 64) & ((i % 128) // 2 == j % 64), 0.125 * scale)
        mid = dot(jnp.concatenate(rows, axis=0), right)
        wide = jnp.concatenate([mid[16 * p : 16 * p + 16] for p in range(4)], axis=1)
        left = ones_where(iota((8, 16), 1) // 2 == iota((8, 16), 0))
        out = dot(left, wide)
        return [out[:, 128 * p : 128 * p + 128] for p in range(4)]

    def send_tile(tiles, pair):
        for offset in NEAR:
            slot = 9 * (1 - offset[0]) + 3 * (1 - offset[1]) + (1 - offset[2])
            send(tiles.at[13], tiles.at[slot], sem1.at[pair], sem1.at[pair + 1], offset)

    def unpack_tile(tiles, put):
        lane = iota((8, 128), 1)
        for i in range(3):
            for j in range(3):
                base = 9 * i + 3 * j
                for p in range(4):
                    own = tiles[base + 1, p]
                    side = jnp.where(lane % 64 < 32, tiles[base + 2, p], tiles[base, p])
                    put(8 * i + p, j, jnp.where(lane < 64, own, roll(side, 64, 1)))
                    put(8 * i + p + 4, j, jnp.where(lane < 64, roll(own, 64, 1), side))

    def restrict_middle(rows, scale):
        i, j = iota((16, 64), 0), iota((16, 64), 1)
        x = 2 * (i // 8) + (i % 8) // 4
        left = ones_where((j // 16 == x) & ((j % 8) // 2 == i % 4))
        mid = dot(left, rows)
        i, j = iota((256, 128), 0), iota((256, 128), 1)
        z = (16 + (i % 128) // 2) % 64
        right = ones_where((i // 128 == j // 64) & (z == j % 64), 0.125 * scale)
        return dot(jnp.concatenate([mid[0:8], mid[8:16]], axis=1), right)

    def send_plane(message, plane, pair):
        slot = gx * 8 + gy
        plane[slot] = message[...]
        for offset in PLANE:
            send(message, plane.at[slot], sem1.at[pair], sem1.at[pair + 1], offset)

    def restrict_plane(load, scale, message):
        i, j = iota((8, 32), 0), iota((8, 32), 1)
        left = ones_where((j // 8 == i // 2) & ((j % 4) // 2 == i % 2))
        i, j = iota((512, 128), 0), iota((512, 128), 1)
        z = i % 64
        right = ones_where(
            (i // 64 == j // 16) & (z >= 16) & (z < 48) & ((z - 16) // 2 == j % 16), 0.125 * scale
        )
        for tile in range(2):
            wide = jnp.concatenate(
                [load(ix)[4 * tile : 4 * tile + 4].reshape(32, 128) for ix in range(4)], axis=1
            )
            message[tile] = dot(dot(left, wide), right)

    def send_ring(message, ring, pair):
        ring[gz] = message[...]
        for offset in RING:
            send(message, ring.at[gz], sem1.at[pair], sem1.at[pair + 1], offset)

    def unpack_ring(ring, out):
        lane = iota((8, 128), 1)
        for x in range(8):
            for tile in range(2):
                acc = jnp.zeros((8, 128), F32)
                for z in range(8):
                    acc = jnp.where(lane // 16 == z, roll(ring[z, tile], 16 * (z - x), 1), acc)
                out[x, 8 * tile : 8 * tile + 8] = acc

    for p, block in enumerate(restrict_fine(lambda x: conductance[x], 0.25)):
        tk[13, p] = block
    send_tile(tk, 0)

    wait_fine(py, recv, sem_r)
    unpack_fine(ea, 3, recv)

    def fine_setup(x):
        inv = make_coefficients(lambda i: ea[1, i], coef0, diag0, inv0, x)
        fi0[x] = ea[2, x] * inv

    planes_loop(1, 23, 2, fine_setup)

    def fine_sweep(load, out, index, first, last, extra=None):
        carry, weight = weights[index]

        def body(x):
            v, r = scaled_residual(load, coef0, fi0, x)
            change = weight * r if index == 0 else carry * w0[x] + weight * r
            w0[x] = change
            out[x] = v + change
            if extra is not None:
                extra(x, v + change)

        planes_loop(first, last, 2, body)

    fine_sweep(lambda i: ea[0, i], va, 0, 1, 23)
    fine_sweep(lambda i: va[i], vb, 1, 2, 22)
    fine_sweep(lambda i: vb[i], va, 2, 3, 21)

    def fine_residual(x):
        v, r = scaled_residual(lambda i: va[i], coef0, fi0, x)
        vb[x] = r * diag0[x]
        ev[0, x, 0:16, 0:128] = v[0:16, 0:128]

    planes_loop(4, 20, 2, fine_residual)
    for p, block in enumerate(restrict_fine(lambda x: vb[4 + x, 0:16, 0:128], 1.0)):
        tf[13, p] = block
    send_tile(tf, 2)

    wait_bytes(tk.at[pl.ds(0, 26)], sem1.at[1])

    def put_k1(x, tile, value):
        k1[x, 8 * tile : 8 * tile + 8] = value

    unpack_tile(tk, put_k1)
    mk[...] = restrict_middle(k1[8:16, 8:16].reshape(64, 128), 0.25)
    send_plane(mk, gk, 4)
    pack_fine(ev, 1, pyv, pzv)
    send_fine(ev, pyv, pzv, recv_v, semv_s, semv_r)

    planes_loop(1, 23, 2, lambda x: make_coefficients(lambda i: k1[i], coef1, diag1, inv1, x))

    wait_bytes(tf.at[pl.ds(0, 26)], sem1.at[3])

    def put_f1(x, tile, value):
        fi1[x, 8 * tile : 8 * tile + 8] = value

    unpack_tile(tf, put_f1)

    def middle_first(x):
        scaled = fi1[x] * inv1[x]
        fi1[x] = scaled
        change = weights[0][1] * scaled
        w1[x] = change
        v1a[x] = change

    planes_loop(1, 23, 2, middle_first)

    def middle_sweep(load, out, index, first, last):
        carry, weight = weights[index]

        def body(x):
            v, r = scaled_residual(load, coef1, fi1, x)
            change = weight * r if index == 0 else carry * w1[x] + weight * r
            w1[x] = change
            out[x] = v + change

        planes_loop(first, last, 2, body)

    middle_sweep(lambda i: v1a[i], v1b, 1, 2, 22)
    middle_sweep(lambda i: v1b[i], v1a, 2, 3, 21)

    def middle_residual(x):
        _, r = scaled_residual(lambda i: v1a[i], coef1, fi1, x)
        v1b[x] = r * diag1[x]

    planes_loop(8, 16, 2, middle_residual)
    mf[...] = restrict_middle(v1b[8:16, 8:16].reshape(64, 128), 1.0)
    send_plane(mf, gf, 6)

    wait_bytes(gk.at[pl.ds(0, 31)], sem1.at[5])
    k2 = gk.reshape(4, 8, 8, 128)
    f2 = gf.reshape(4, 8, 8, 128)
    restrict_plane(lambda ix: k2[ix], 0.25, ck.at[8])
    send_ring(ck.at[8], ck, 8)
    for ix in range(4):
        k, around = shifts_plane(k2, ix)
        faces = [0.5 * (k + other) for other in around]
        d = SHIFT + ((faces[0] + faces[1]) + (faces[2] + faces[3]) + (faces[4] + faces[5]))
        inv = 1.0 / d
        for n in range(6):
            coef2[n, ix] = faces[n] * inv
        diag2[ix] = d
        inv2[ix] = inv

    wait_bytes(gf.at[pl.ds(0, 31)], sem1.at[7])
    for ix in range(4):
        change = weights[0][1] * (f2[ix] * inv2[ix])
        w2[ix] = change
        v2a[ix] = change

    def plane_residual(ref, ix):
        v, around = shifts_plane(ref, ix)
        total = f2[ix] * inv2[ix] - v
        for n in range(6):
            total = total + coef2[n, ix] * around[n]
        return v, total

    def plane_sweep(ref, out, index):
        carry, weight = weights[index]
        for ix in range(4):
            v, r = plane_residual(ref, ix)
            change = weight * r if index == 0 else carry * w2[ix] + weight * r
            w2[ix] = change
            out[ix] = v + change

    plane_sweep(v2a, v2b, 1)
    plane_sweep(v2b, v2a, 2)
    for ix in range(4):
        v2b[ix] = plane_residual(v2a, ix)[1] * diag2[ix]
    restrict_plane(lambda ix: v2b[ix], 1.0, cf.at[8])
    send_ring(cf.at[8], cf, 10)

    wait_bytes(ck.at[pl.ds(0, 7)], sem1.at[9])
    unpack_ring(ck, k3)
    for x in range(8):
        k = k3[x]
        faces = [0.5 * (k + k3[(x + 1) % 8]), 0.5 * (k + k3[(x + 7) % 8])]
        faces += [0.5 * (k + roll(k, s, dim)) for dim in (0, 1) for s in (-1, 1)]
        d = SHIFT + ((faces[0] + faces[1]) + (faces[2] + faces[3]) + (faces[4] + faces[5]))
        inv = 1.0 / d
        for n in range(6):
            coef3[n, x] = faces[n] * inv
        coef3[6, x] = inv
    wait_bytes(cf.at[pl.ds(0, 7)], sem1.at[11])
    unpack_ring(cf, f3)
    for x in range(8):
        scaled = f3[x] * coef3[6, x]
        f3[x] = scaled
        change = coarse_weights[0][1] * scaled
        w3[x] = change
        v3a[x] = change
    bufs = (v3a, v3b)
    for index in range(1, COARSE_ITERS):
        old, new = bufs[(index + 1) % 2], bufs[index % 2]
        carry, weight = coarse_weights[index]
        for x in range(8):
            v = old[x]
            total = f3[x] - v
            total = total + (coef3[0, x] * old[(x + 1) % 8] + coef3[1, x] * old[(x + 7) % 8])
            total = total + (coef3[2, x] * roll(v, -1, 0) + coef3[3, x] * roll(v, 1, 0))
            total = total + (coef3[4, x] * roll(v, -1, 1) + coef3[5, x] * roll(v, 1, 1))
            change = carry * w3[x] + weight * total
            w3[x] = change
            new[x] = v + change
    v3 = bufs[(COARSE_ITERS - 1) % 2]

    i, j = iota((256, 128), 0), iota((256, 128), 1)
    z = lax.rem(16 * gz + 120 + (j % 64) // 2, 128)
    right = ones_where((i // 128 == j // 64) & (i % 128 == z))
    rows = jnp.concatenate(
        [jnp.concatenate([v3[2 * ix], v3[2 * ix + 1]], axis=1) for ix in range(4)], axis=0
    )
    mid = dot(rows, right)
    wide = jnp.concatenate([mid[16 * ix : 16 * ix + 16] for ix in range(4)], axis=1)
    i, j = iota((64, 16), 0), iota((64, 16), 1)
    left = ones_where(j == 2 * (i // 8) + (i % 4) // 2)
    spread = dot(left, wide)
    for ix in range(4):
        v2b[ix] = v2a[ix] + spread[:, 128 * ix : 128 * ix + 128].reshape(8, 8, 128)
    plane_sweep(v2b, v2a, 0)
    plane_sweep(v2a, v2b, 1)
    plane_sweep(v2b, v2a, 2)

    tiles = [
        v2a[lax.rem(gx + i + 3, 4), lax.rem(gy + j + 7, 8)] for i in range(3) for j in range(3)
    ]
    i, j = iota((128, 256), 0), iota((128, 256), 1)
    right = ones_where((i // 64 == j // 128) & (i % 64 == (16 + (j % 128) // 2) % 64))
    mid = dot(jnp.concatenate(tiles, axis=0), right)
    wide = jnp.concatenate([mid[8 * t : 8 * t + 8] for t in range(9)], axis=1)
    i, j = iota((32, 8), 0), iota((32, 8), 1)
    left = ones_where(j == (i // 16) * 4 + (i % 8) // 2)
    spread = dot(left, wide)
    for t in range(9):
        for h in range(2):
            for x in range(4):
                plane = 8 * (t // 3) + 4 * h + x
                at = 8 * (t % 3)
                v1b[plane, at : at + 8] = (
                    v1a[plane, at : at + 8]
                    + spread[8 * x : 8 * x + 8, 256 * t + 128 * h : 256 * t + 128 * h + 128]
                )
    middle_sweep(lambda i: v1b[i], v1a, 0, 4, 20)
    middle_sweep(lambda i: v1a[i], v1b, 1, 5, 19)
    middle_sweep(lambda i: v1b[i], v1a, 2, 6, 18)

    wait_fine(pyv, recv_v, semv_r)
    unpack_fine(ev, 1, recv_v)
    wide = jnp.concatenate([v1a[6 + p] for p in range(12)], axis=1)
    i, j = iota((24, 24), 0), iota((24, 24), 1)
    left = ones_where(j == jnp.where(i < 20, 8 + i // 2, i // 2 - 4))
    mid = dot(left, wide)
    i, j = iota((128, 256), 0), iota((128, 256), 1)
    right = ones_where(i == j // 2)
    spread = dot(jnp.concatenate([mid[:, 128 * p : 128 * p + 128] for p in range(12)], axis=0), right)
    for p in range(12):
        for u in range(2):
            va[2 * p + u] = ev[0, 2 * p + u] + spread[24 * p : 24 * p + 24]
    fine_sweep(lambda i: va[i], vb, 0, 1, 23)
    fine_sweep(lambda i: vb[i], va, 1, 2, 22)
    fine_sweep(lambda i: va[i], vb, 2, 3, 21)

    def fine_last(x):
        v, r = scaled_residual(lambda i: vb[i], coef0, fi0, x)
        pressure[x - 4] = v[0:16, 0:128]
        residual[x - 4] = (r * diag0[x])[0:16, 0:128]

    planes_loop(4, 20, 2, fine_last)

    wait_fine(py, recv, sem_s)
    wait_fine(pyv, recv_v, semv_s)
    wait_bytes(tk.at[pl.ds(0, 26)], sem1.at[0])
    wait_bytes(tf.at[pl.ds(0, 26)], sem1.at[2])
    wait_bytes(gk.at[pl.ds(0, 31)], sem1.at[4])
    wait_bytes(gf.at[pl.ds(0, 31)], sem1.at[6])
    wait_bytes(ck.at[pl.ds(0, 7)], sem1.at[8])
    wait_bytes(cf.at[pl.ds(0, 7)], sem1.at[10])


def vmem(*shape):
    return pltpu.VMEM(shape, F32)


def fine_buffers(count):
    return [
        vmem(2, count, 8, 8, 128), vmem(2, count, 2, 8, 128), vmem(2, 2, count, 2, 8, 128),
        vmem(2, 2, count, 2, 8, 128), vmem(2, 2, count, 8, 128), vmem(2, 2, 2, count, 8, 128),
    ]


def per_device(source, conductance, pressure_start):
    fine = (24, 24, 256)
    middle = (24, 24, 128)
    plane = (4, 8, 8, 128)
    coarse = (8, 16, 128)
    scratch = [
        vmem(3, *fine), vmem(1, *fine), vmem(*fine), vmem(*fine), vmem(*fine), vmem(*fine),
        vmem(6, *fine), vmem(*fine), vmem(*fine),
        vmem(2, 3, 8, 8, 128), vmem(3, 2, 8, 128), vmem(2, 1, 8, 8, 128), vmem(1, 2, 8, 128),
    ]
    scratch += fine_buffers(3) + fine_buffers(1)
    scratch += [
        vmem(27, 4, 8, 128), vmem(27, 4, 8, 128), vmem(*middle), vmem(*middle), vmem(*middle),
        vmem(*middle), vmem(*middle), vmem(6, *middle), vmem(*middle), vmem(*middle),
        vmem(32, 8, 128), vmem(32, 8, 128), vmem(8, 128), vmem(8, 128),
        vmem(*plane), vmem(*plane), vmem(*plane), vmem(6, *plane), vmem(*plane), vmem(*plane),
        vmem(9, 2, 8, 128), vmem(9, 2, 8, 128), vmem(*coarse), vmem(*coarse), vmem(*coarse),
        vmem(*coarse), vmem(*coarse), vmem(7, *coarse),
        pltpu.SemaphoreType.DMA((7,)), pltpu.SemaphoreType.DMA((7,)),
        pltpu.SemaphoreType.DMA((7,)), pltpu.SemaphoreType.DMA((7,)),
        pltpu.SemaphoreType.DMA((12,)),
    ]
    block = jax.ShapeDtypeStruct(source.shape, F32)
    whole = pl.BlockSpec(memory_space=pltpu.VMEM)
    return pl.pallas_call(
        kernel,
        out_shape=(block, block),
        in_specs=[whole] * 3,
        out_specs=(whole, whole),
        scratch_shapes=scratch,
        compiler_params=pltpu.CompilerParams(
            collective_id=0, has_side_effects=True, vmem_limit_bytes=48 * 1024 * 1024
        ),
    )(source, conductance, pressure_start)


def solution(mesh):
    placed = (P("gx", "gy", "gz"), P("gx", "gy", "gz"), P("gx", "gy", "gz"))
    return jax.shard_map(
        per_device,
        mesh=mesh,
        in_specs=placed,
        out_specs=(P("gx", "gy", "gz"), P("gx", "gy", "gz")),
        check_vma=False,
    )
```

time: 524 us -> 62.4 us (0.12)
  the two profiles are of different devices: /device:TPU:6 before, /device:TPU:1 now
where the time goes in v1:
time: 62.4 us; the launch traced here: 62.3 us
  Pallas kernels  57.6 us (92%)
  local copies, waits for them, and re-layouts  4.02 us (6%)
  between operations  0.65 us (1%)
    pallas_call x1, Pallas kernels, per_device(): pl.pallas_call(kernel, out_shape=(block, block), in_specs=[whole] * 3, ou...  57.6 us
    unnamed x8, local copies, waits for them, and re-layouts  4.02 us

profile of v1, /device:TPU:1, one launch (start us, length us, event | category | flops | bytes accessed | tf_op | source)
XLA Modules:
  0.0 62.3 jit_solution(16849613042376300995)
XLA Ops:
  0.6 0.0 copy-start
  0.6 0.9 %copy-done = f32[16,16,128]{2,1,0:T(8,128)S(1)} copy-done((f32[16,16,128]{2,1,0:T(8,128)S(1)}, f32[16,16,128]{2,1,0:T(8,128)}, u32[]{:S(2)}) %copy-start) | copy-done | bytes 131096
  1.5 0.0 copy-start.1
  1.5 0.9 %copy-done.1 = f32[16,16,128]{2,1,0:T(8,128)S(1)} copy-done((f32[16,16,128]{2,1,0:T(8,128)S(1)}, f32[16,16,128]{2,1,0:T(8,128)}, u32[]{:S(2)}) %copy-start.1) | copy-done | bytes 131096
  2.4 0.0 copy-start.2
  2.4 0.9 %copy-done.2 = f32[16,16,128]{2,1,0:T(8,128)S(1)} copy-done((f32[16,16,128]{2,1,0:T(8,128)S(1)}, f32[16,16,128]{2,1,0:T(8,128)}, u32[]{:S(2)}) %copy-start.2) | copy-done | bytes 131096
  3.3 57.6 %shard_map.50 = (f32[16,16,128]{2,1,0:T(8,128)S(1)}, f32[16,16,128]{2,1,0:T(8,128)S(1)}) custom-call(f32[16,16,128]{2,1,0:T(8,128)S(1)} %copy-done, f32[16,16,128]{2,1,0:T(8,128)S(1)} %copy-done.1, f32[16,16,128]{2,1,0:T(8,128)S(1)} %copy-done.2), custom_call_target="tpu_custom_call" | custom-call | tf_op jit(solution)/shard_map/pallas_call | solution.py:608
  61.0 0.7 %copy.7 = f32[16,16,128]{2,1,0:T(8,128)} copy(f32[16,16,128]{2,1,0:T(8,128)S(1)} %get-tuple-element.4) | data formatting | bytes 262144
  61.6 0.7 %copy.8 = f32[16,16,128]{2,1,0:T(8,128)} copy(f32[16,16,128]{2,1,0:T(8,128)S(1)} %get-tuple-element.5) | data formatting | bytes 262144
Async XLA Ops:
  0.6 0.9 %copy-start = (f32[16,16,128]{2,1,0:T(8,128)S(1)}, f32[16,16,128]{2,1,0:T(8,128)}, u32[]{:S(2)}) copy-start(f32[16,16,128]{2,1,0:T(8,128)} %source.1) | copy-start | bytes 393220
  1.5 0.9 %copy-start.1 = (f32[16,16,128]{2,1,0:T(8,128)S(1)}, f32[16,16,128]{2,1,0:T(8,128)}, u32[]{:S(2)}) copy-start(f32[16,16,128]{2,1,0:T(8,128)} %conductance.1) | copy-start | bytes 393220
  2.4 0.9 %copy-start.2 = (f32[16,16,128]{2,1,0:T(8,128)S(1)}, f32[16,16,128]{2,1,0:T(8,128)}, u32[]{:S(2)}) copy-start(f32[16,16,128]{2,1,0:T(8,128)} %start.1) | copy-start | bytes 393220

commit v2 on v1

--- a/solution.py
+++ b/solution.py
@@ -174,17 +174,9 @@
                     ext[a, plane, 8 * tile : 8 * tile + 8, 128:256] = roll(comb, -(8 * x + 4), 1)
 
 
-def planes_loop(first, last, unroll, body):
-    total = last - first
-    while total % unroll:
-        unroll -= 1
-
-    def step(i, carry):
-        for u in range(unroll):
-            body(first + i * unroll + u)
-        return carry
-
-    lax.fori_loop(0, total // unroll, step, 0)
+def planes_loop(first, last, body):
+    for x in range(first, last):
+        body(x)
 
 
 def make_coefficients(load, coef, diag, inverse, x):
@@ -230,17 +222,20 @@
 
 def kernel(
     source, conductance, start, pressure, residual,
-    ea, ev, va, vb, w0, fi0, coef0, diag0, inv0, py, pz, pyv, pzv,
+    m_fine, m_middle, m_coarse, m_plane, m_tile, m_spread,
+    ek, ea, ev, va, vb, w0, fi0, coef0, diag0, inv0, pyk, pzk, py, pz, pyv, pzv,
+    ryk, rzk, rxyk, rxzk, ryzk, rxyzk,
     ry, rz, rxy, rxz, ryz, rxyz, ryv, rzv, rxyv, rxzv, ryzv, rxyzv,
     tk, tf, k1, v1a, v1b, w1, fi1, coef1, diag1, inv1,
     gk, gf, mk, mf, v2a, v2b, w2, coef2, diag2, inv2,
     ck, cf, k3, f3, v3a, v3b, w3, coef3,
-    sem_s, sem_r, semv_s, semv_r, sem1,
+    sem_in, semk_s, semk_r, sem_s, sem_r, semv_s, semv_r, sem1,
 ):
     weights = chebyshev_weights(DEG, SMOOTH_FLOOR)
     coarse_weights = chebyshev_weights(COARSE_ITERS, COARSE_FLOOR)
     gx, gy, gz = (lax.axis_index(axis) for axis in AXES)
     recv = (ry, rz, rxy, rxz, ryz, rxyz)
+    recv_k = (ryk, rzk, rxyk, rxzk, ryzk, rxyzk)
     recv_v = (ryv, rzv, rxyv, rxzv, ryzv, rxyzv)
 
     everyone = list(dict.fromkeys(
@@ -250,24 +245,42 @@
     for offset in everyone:
         pl.semaphore_signal(barrier, inc=1, device_id=peer(offset), device_id_type=MESH)
 
-    for a, ref in enumerate((start, conductance, source)):
-        ea[a, 4:20, 0:16, 0:128] = ref[...]
-    pack_fine(ea, 3, py, pz)
-    pl.semaphore_wait(barrier, len(everyone))
-    send_fine(ea, py, pz, recv, sem_s, sem_r)
+    own = (pl.ds(4, 16), pl.ds(0, 16), pl.ds(0, 128))
+    inputs = [
+        pltpu.make_async_copy(ref, to.at[own], sem_in.at[n])
+        for n, (ref, to) in enumerate(
+            ((conductance, ek.at[0]), (start, ea.at[0]), (source, ea.at[1]))
+        )
+    ]
+    for copy in inputs:
+        copy.start()
+
+    i, j = iota((256, 128), 0), iota((256, 128), 1)
+    m_fine[...] = ones_where((i // 128 == j // 64) & ((i % 128) // 2 == j % 64), 0.125)
+    m_middle[...] = ones_where(
+        (i // 128 == j // 64) & ((16 + (i % 128) // 2) % 64 == j % 64), 0.125
+    )
+    z = lax.rem(16 * gz + 120 + (j % 64) // 2, 128)
+    m_coarse[...] = ones_where((i // 128 == j // 64) & (i % 128 == z))
+    i, j = iota((512, 128), 0), iota((512, 128), 1)
+    z = i % 64
+    m_plane[...] = ones_where(
+        (i // 64 == j // 16) & (z >= 16) & (z < 48) & ((z - 16) // 2 == j % 16), 0.125
+    )
+    i, j = iota((128, 256), 0), iota((128, 256), 1)
+    m_tile[...] = ones_where((i // 64 == j // 128) & (i % 64 == (16 + (j % 128) // 2) % 64))
+    m_spread[...] = ones_where(i == j // 2)
 
     def restrict_fine(load, scale):
         rows = [
             jnp.concatenate([load(2 * p) + load(2 * p + 1), load(2 * p + 8) + load(2 * p + 9)], axis=1)
             for p in range(4)
         ]
-        i, j = iota((256, 128), 0), iota((256, 128), 1)
-        right = ones_where((i // 128 == j // 64) & ((i % 128) // 2 == j % 64), 0.125 * scale)
-        mid = dot(jnp.concatenate(rows, axis=0), right)
+        mid = dot(jnp.concatenate(rows, axis=0), m_fine[...])
         wide = jnp.concatenate([mid[16 * p : 16 * p + 16] for p in range(4)], axis=1)
         left = ones_where(iota((8, 16), 1) // 2 == iota((8, 16), 0))
         out = dot(left, wide)
-        return [out[:, 128 * p : 128 * p + 128] for p in range(4)]
+        return [scale * out[:, 128 * p : 128 * p + 128] for p in range(4)]
 
     def send_tile(tiles, pair):
         for offset in NEAR:
@@ -290,10 +303,7 @@
         x = 2 * (i // 8) + (i % 8) // 4
         left = ones_where((j // 16 == x) & ((j % 8) // 2 == i % 4))
         mid = dot(left, rows)
-        i, j = iota((256, 128), 0), iota((256, 128), 1)
-        z = (16 + (i % 128) // 2) % 64
-        right = ones_where((i // 128 == j // 64) & (z == j % 64), 0.125 * scale)
-        return dot(jnp.concatenate([mid[0:8], mid[8:16]], axis=1), right)
+        return scale * dot(jnp.concatenate([mid[0:8], mid[8:16]], axis=1), m_middle[...])
 
     def send_plane(message, plane, pair):
         slot = gx * 8 + gy
@@ -304,16 +314,11 @@
     def restrict_plane(load, scale, message):
         i, j = iota((8, 32), 0), iota((8, 32), 1)
         left = ones_where((j // 8 == i // 2) & ((j % 4) // 2 == i % 2))
-        i, j = iota((512, 128), 0), iota((512, 128), 1)
-        z = i % 64
-        right = ones_where(
-            (i // 64 == j // 16) & (z >= 16) & (z < 48) & ((z - 16) // 2 == j % 16), 0.125 * scale
-        )
         for tile in range(2):
             wide = jnp.concatenate(
                 [load(ix)[4 * tile : 4 * tile + 4].reshape(32, 128) for ix in range(4)], axis=1
             )
-            message[tile] = dot(dot(left, wide), right)
+            message[tile] = scale * dot(dot(left, wide), m_plane[...])
 
     def send_ring(message, ring, pair):
         ring[gz] = message[...]
@@ -329,18 +334,28 @@
                     acc = jnp.where(lane // 16 == z, roll(ring[z, tile], 16 * (z - x), 1), acc)
                 out[x, 8 * tile : 8 * tile + 8] = acc
 
-    for p, block in enumerate(restrict_fine(lambda x: conductance[x], 0.25)):
+    inputs[0].wait()
+    pack_fine(ek, 1, pyk, pzk)
+    for p, block in enumerate(restrict_fine(lambda x: ek[0, 4 + x, 0:16, 0:128], 0.25)):
         tk[13, p] = block
+    inputs[1].wait()
+    inputs[2].wait()
+    pack_fine(ea, 2, py, pz)
+    pl.semaphore_wait(barrier, len(everyone))
+    send_fine(ek, pyk, pzk, recv_k, semk_s, semk_r)
+    send_fine(ea, py, pz, recv, sem_s, sem_r)
+
+    wait_fine(pyk, recv_k, semk_r)
+    unpack_fine(ek, 1, recv_k)
+    planes_loop(1, 23, lambda x: make_coefficients(lambda i: ek[0, i], coef0, diag0, inv0, x))
+    wait_fine(py, recv, sem_r)
     send_tile(tk, 0)
-
-    wait_fine(py, recv, sem_r)
-    unpack_fine(ea, 3, recv)
-
-    def fine_setup(x):
-        inv = make_coefficients(lambda i: ea[1, i], coef0, diag0, inv0, x)
-        fi0[x] = ea[2, x] * inv
-
-    planes_loop(1, 23, 2, fine_setup)
+    unpack_fine(ea, 2, recv)
+
+    def fine_scale(x):
+        fi0[x] = ea[1, x] * inv0[x]
+
+    planes_loop(1, 23, fine_scale)
 
     def fine_sweep(load, out, index, first, last, extra=None):
         carry, weight = weights[index]
@@ -353,7 +368,7 @@
             if extra is not None:
                 extra(x, v + change)
 
-        planes_loop(first, last, 2, body)
+        planes_loop(first, last, body)
 
     fine_sweep(lambda i: ea[0, i], va, 0, 1, 23)
     fine_sweep(lambda i: va[i], vb, 1, 2, 22)
@@ -364,7 +379,7 @@
         vb[x] = r * diag0[x]
         ev[0, x, 0:16, 0:128] = v[0:16, 0:128]
 
-    planes_loop(4, 20, 2, fine_residual)
+    planes_loop(4, 20, fine_residual)
     for p, block in enumerate(restrict_fine(lambda x: vb[4 + x, 0:16, 0:128], 1.0)):
         tf[13, p] = block
     send_tile(tf, 2)
@@ -377,10 +392,7 @@
     unpack_tile(tk, put_k1)
     mk[...] = restrict_middle(k1[8:16, 8:16].reshape(64, 128), 0.25)
     send_plane(mk, gk, 4)
-    pack_fine(ev, 1, pyv, pzv)
-    send_fine(ev, pyv, pzv, recv_v, semv_s, semv_r)
-
-    planes_loop(1, 23, 2, lambda x: make_coefficients(lambda i: k1[i], coef1, diag1, inv1, x))
+    planes_loop(1, 23, lambda x: make_coefficients(lambda i: k1[i], coef1, diag1, inv1, x))
 
     wait_bytes(tf.at[pl.ds(0, 26)], sem1.at[3])
 
@@ -396,7 +408,7 @@
         w1[x] = change
         v1a[x] = change
 
-    planes_loop(1, 23, 2, middle_first)
+    planes_loop(1, 23, middle_first)
 
     def middle_sweep(load, out, index, first, last):
         carry, weight = weights[index]
@@ -407,7 +419,7 @@
             w1[x] = change
             out[x] = v + change
 
-        planes_loop(first, last, 2, body)
+        planes_loop(first, last, body)
 
     middle_sweep(lambda i: v1a[i], v1b, 1, 2, 22)
     middle_sweep(lambda i: v1b[i], v1a, 2, 3, 21)
@@ -416,9 +428,11 @@
         _, r = scaled_residual(lambda i: v1a[i], coef1, fi1, x)
         v1b[x] = r * diag1[x]
 
-    planes_loop(8, 16, 2, middle_residual)
+    planes_loop(8, 16, middle_residual)
     mf[...] = restrict_middle(v1b[8:16, 8:16].reshape(64, 128), 1.0)
     send_plane(mf, gf, 6)
+    pack_fine(ev, 1, pyv, pzv)
+    send_fine(ev, pyv, pzv, recv_v, semv_s, semv_r)
 
     wait_bytes(gk.at[pl.ds(0, 31)], sem1.at[5])
     k2 = gk.reshape(4, 8, 8, 128)
@@ -497,13 +511,10 @@
             new[x] = v + change
     v3 = bufs[(COARSE_ITERS - 1) % 2]
 
-    i, j = iota((256, 128), 0), iota((256, 128), 1)
-    z = lax.rem(16 * gz + 120 + (j % 64) // 2, 128)
-    right = ones_where((i // 128 == j // 64) & (i % 128 == z))
     rows = jnp.concatenate(
         [jnp.concatenate([v3[2 * ix], v3[2 * ix + 1]], axis=1) for ix in range(4)], axis=0
     )
-    mid = dot(rows, right)
+    mid = dot(rows, m_coarse[...])
     wide = jnp.concatenate([mid[16 * ix : 16 * ix + 16] for ix in range(4)], axis=1)
     i, j = iota((64, 16), 0), iota((64, 16), 1)
     left = ones_where(j == 2 * (i // 8) + (i % 4) // 2)
@@ -517,9 +528,7 @@
     tiles = [
         v2a[lax.rem(gx + i + 3, 4), lax.rem(gy + j + 7, 8)] for i in range(3) for j in range(3)
     ]
-    i, j = iota((128, 256), 0), iota((128, 256), 1)
-    right = ones_where((i // 64 == j // 128) & (i % 64 == (16 + (j % 128) // 2) % 64))
-    mid = dot(jnp.concatenate(tiles, axis=0), right)
+    mid = dot(jnp.concatenate(tiles, axis=0), m_tile[...])
     wide = jnp.concatenate([mid[8 * t : 8 * t + 8] for t in range(9)], axis=1)
     i, j = iota((32, 8), 0), iota((32, 8), 1)
     left = ones_where(j == (i // 16) * 4 + (i % 8) // 2)
@@ -543,9 +552,9 @@
     i, j = iota((24, 24), 0), iota((24, 24), 1)
     left = ones_where(j == jnp.where(i < 20, 8 + i // 2, i // 2 - 4))
     mid = dot(left, wide)
-    i, j = iota((128, 256), 0), iota((128, 256), 1)
-    right = ones_where(i == j // 2)
-    spread = dot(jnp.concatenate([mid[:, 128 * p : 128 * p + 128] for p in range(12)], axis=0), right)
+    spread = dot(
+        jnp.concatenate([mid[:, 128 * p : 128 * p + 128] for p in range(12)], axis=0), m_spread[...]
+    )
     for p in range(12):
         for u in range(2):
             va[2 * p + u] = ev[0, 2 * p + u] + spread[24 * p : 24 * p + 24]
@@ -558,8 +567,9 @@
         pressure[x - 4] = v[0:16, 0:128]
         residual[x - 4] = (r * diag0[x])[0:16, 0:128]
 
-    planes_loop(4, 20, 2, fine_last)
-
+    planes_loop(4, 20, fine_last)
+
+    wait_fine(pyk, recv_k, semk_s)
     wait_fine(py, recv, sem_s)
     wait_fine(pyv, recv_v, semv_s)
     wait_bytes(tk.at[pl.ds(0, 26)], sem1.at[0])
@@ -587,11 +597,12 @@
     plane = (4, 8, 8, 128)
     coarse = (8, 16, 128)
     scratch = [
-        vmem(3, *fine), vmem(1, *fine), vmem(*fine), vmem(*fine), vmem(*fine), vmem(*fine),
+        vmem(256, 128), vmem(256, 128), vmem(256, 128), vmem(512, 128), vmem(128, 256), vmem(128, 256),
+        vmem(1, *fine), vmem(2, *fine), vmem(1, *fine), vmem(*fine), vmem(*fine), vmem(*fine), vmem(*fine),
         vmem(6, *fine), vmem(*fine), vmem(*fine),
-        vmem(2, 3, 8, 8, 128), vmem(3, 2, 8, 128), vmem(2, 1, 8, 8, 128), vmem(1, 2, 8, 128),
+        vmem(2, 1, 8, 8, 128), vmem(1, 2, 8, 128), vmem(2, 2, 8, 8, 128), vmem(2, 2, 8, 128), vmem(2, 1, 8, 8, 128), vmem(1, 2, 8, 128),
     ]
-    scratch += fine_buffers(3) + fine_buffers(1)
+    scratch += fine_buffers(1) + fine_buffers(2) + fine_buffers(1)
     scratch += [
         vmem(27, 4, 8, 128), vmem(27, 4, 8, 128), vmem(*middle), vmem(*middle), vmem(*middle),
         vmem(*middle), vmem(*middle), vmem(6, *middle), vmem(*middle), vmem(*middle),
@@ -599,6 +610,8 @@
         vmem(*plane), vmem(*plane), vmem(*plane), vmem(6, *plane), vmem(*plane), vmem(*plane),
         vmem(9, 2, 8, 128), vmem(9, 2, 8, 128), vmem(*coarse), vmem(*coarse), vmem(*coarse),
         vmem(*coarse), vmem(*coarse), vmem(7, *coarse),
+        pltpu.SemaphoreType.DMA((3,)),
+        pltpu.SemaphoreType.DMA((7,)), pltpu.SemaphoreType.DMA((7,)),
         pltpu.SemaphoreType.DMA((7,)), pltpu.SemaphoreType.DMA((7,)),
         pltpu.SemaphoreType.DMA((7,)), pltpu.SemaphoreType.DMA((7,)),
         pltpu.SemaphoreType.DMA((12,)),
@@ -608,7 +621,7 @@
     return pl.pallas_call(
         kernel,
         out_shape=(block, block),
-        in_specs=[whole] * 3,
+        in_specs=[pl.BlockSpec(memory_space=pltpu.HBM)] * 3,
         out_specs=(whole, whole),
         scratch_shapes=scratch,
         compiler_params=pltpu.CompilerParams(

time: 62.4 us -> 49.2 us (0.79)
  Pallas kernels: 57.6 us -> 44.4 us
    pallas_call x1, Pallas kernels: 57.6 us -> 44.4 us  [per_device(): pl.pallas_call(kernel, out_shape=(block, block), in_specs=[pl.BlockSpec(m...]
where the time goes in v2:
time: 49.2 us; the launch traced here: 49 us
  Pallas kernels  44.4 us (90%)
  local copies, waits for them, and re-layouts  4.02 us (8%)
  between operations  0.65 us (1%)
    pallas_call x1, Pallas kernels, per_device(): pl.pallas_call(kernel, out_shape=(block, block), in_specs=[pl.BlockSpec(m...  44.4 us
    unnamed x8, local copies, waits for them, and re-layouts  4.02 us

profile of v2, /device:TPU:1, one launch (start us, length us, event | category | flops | bytes accessed | tf_op | source)
XLA Modules:
  0.0 49.0 jit_solution(6037485684706127377)
XLA Ops:
  0.6 0.0 copy-start
  0.6 0.9 %copy-done = f32[16,16,128]{2,1,0:T(8,128)S(1)} copy-done((f32[16,16,128]{2,1,0:T(8,128)S(1)}, f32[16,16,128]{2,1,0:T(8,128)}, u32[]{:S(2)}) %copy-start) | copy-done | bytes 131096
  1.5 0.0 copy-start.1
  1.5 0.9 %copy-done.1 = f32[16,16,128]{2,1,0:T(8,128)S(1)} copy-done((f32[16,16,128]{2,1,0:T(8,128)S(1)}, f32[16,16,128]{2,1,0:T(8,128)}, u32[]{:S(2)}) %copy-start.1) | copy-done | bytes 131096
  2.4 0.0 copy-start.2
  2.4 0.9 %copy-done.2 = f32[16,16,128]{2,1,0:T(8,128)S(1)} copy-done((f32[16,16,128]{2,1,0:T(8,128)S(1)}, f32[16,16,128]{2,1,0:T(8,128)}, u32[]{:S(2)}) %copy-start.2) | copy-done | bytes 131096
  3.3 44.4 %shard_map.50 = (f32[16,16,128]{2,1,0:T(8,128)S(1)}, f32[16,16,128]{2,1,0:T(8,128)S(1)}) custom-call(f32[16,16,128]{2,1,0:T(8,128)S(1)} %copy-done, f32[16,16,128]{2,1,0:T(8,128)S(1)} %copy-done.1, f32[16,16,128]{2,1,0:T(8,128)S(1)} %copy-done.2), custom_call_target="tpu_custom_call" | custom-call | tf_op jit(solution)/shard_map/pallas_call | solution.py:621
  47.7 0.7 %copy.7 = f32[16,16,128]{2,1,0:T(8,128)} copy(f32[16,16,128]{2,1,0:T(8,128)S(1)} %get-tuple-element.4) | data formatting | bytes 262144
  48.4 0.7 %copy.8 = f32[16,16,128]{2,1,0:T(8,128)} copy(f32[16,16,128]{2,1,0:T(8,128)S(1)} %get-tuple-element.5) | data formatting | bytes 262144
Async XLA Ops:
  0.6 0.9 %copy-start = (f32[16,16,128]{2,1,0:T(8,128)S(1)}, f32[16,16,128]{2,1,0:T(8,128)}, u32[]{:S(2)}) copy-start(f32[16,16,128]{2,1,0:T(8,128)} %source.1) | copy-start | bytes 393220
  1.5 0.9 %copy-start.1 = (f32[16,16,128]{2,1,0:T(8,128)S(1)}, f32[16,16,128]{2,1,0:T(8,128)}, u32[]{:S(2)}) copy-start(f32[16,16,128]{2,1,0:T(8,128)} %conductance.1) | copy-start | bytes 393220
  2.4 0.9 %copy-start.2 = (f32[16,16,128]{2,1,0:T(8,128)S(1)}, f32[16,16,128]{2,1,0:T(8,128)}, u32[]{:S(2)}) copy-start(f32[16,16,128]{2,1,0:T(8,128)} %start.1) | copy-start | bytes 393220

commit v3 on v2

--- a/solution.py
+++ b/solution.py
@@ -79,7 +79,7 @@
     pltpu.make_async_copy(ref, ref, sem).wait()
 
 
-def pack_fine(ext, count, py, pz):
+def pack_fine(ext, count, py, pz, pw):
     sub = iota((8, 128), 0)
     lane = iota((8, 128), 1)
     for a in range(count):
@@ -99,9 +99,18 @@
                 row = ext[a, 4 + x, 8 * tile : 8 * tile + 8, 0:128]
                 acc = jnp.where(lane // 8 == x, roll(row, 8 * x + 4, 1), acc)
             pz[a, tile] = acc
-
-
-def send_fine(ext, py, pz, recv, ssem, rsem):
+    for side in range(2):
+        acc = jnp.zeros((8, 128), F32)
+        for a in range(count):
+            for tile in range(2):
+                at = 2 * a + tile
+                acc = jnp.where(
+                    lane // 32 == at, roll(pz[a, tile], 32 * at - (0 if side else 96), 1), acc
+                )
+        pw[side] = acc
+
+
+def send_fine(ext, py, pz, pw, recv, ssem, rsem):
     ry, rz, rxy, rxz, ryz, rxyz = recv
     for offset in NEAR:
         dx, dy, dz = offset
@@ -120,11 +129,11 @@
         elif kind == (True, True, False):
             src, dst, which = py.at[yi, :, planes], rxy.at[xi, yi], 3
         elif kind == (True, False, True):
-            src, dst, which = pz, rxz.at[xi, zi], 4
+            src, dst, which = pw.at[xi], rxz.at[xi, zi], 4
         elif kind == (False, True, True):
             src, dst, which = pz.at[:, tile], ryz.at[yi, zi], 5
         else:
-            src, dst, which = pz.at[:, tile], rxyz.at[xi, yi, zi], 6
+            src, dst, which = pw.at[xi], rxyz.at[xi, yi, zi], 6
         send(src, dst, ssem.at[which], rsem.at[which], offset)
 
 
@@ -153,25 +162,28 @@
         for r in range(2):
             place(a, r, rxy[0, 0, a, r], rxy[0, 1, a, r])
             place(a, 20 + r, rxy[1, 0, a, r], rxy[1, 1, a, r])
-        for part in range(3):
+        for tile in range(3):
+            both = []
+            for zi in range(2):
+                if tile < 2:
+                    both.append(rz[zi, a, tile])
+                else:
+                    both.append(jnp.where(low, ryz[1, zi, a], ryz[0, zi, a]))
+            comb = jnp.where(zleft, both[0], both[1])
+            for x in range(16):
+                ext[a, 4 + x, 8 * tile : 8 * tile + 8, 128:256] = roll(comb, -(8 * x + 4), 1)
+    for side in range(2):
+        edge = jnp.where(zleft, rxz[side, 0], rxz[side, 1])
+        left = jnp.where(zleft, rxyz[side, 0, 0], rxyz[side, 0, 1])
+        right = jnp.where(zleft, rxyz[side, 1, 0], rxyz[side, 1, 1])
+        corner = jnp.where(low, right, roll(left, -32, 1))
+        for a in range(count):
             for tile in range(3):
-                both = []
-                for zi in range(2):
-                    if tile < 2:
-                        both.append(rz[zi, a, tile] if part == 0 else rxz[part - 1, zi, a, tile])
-                    elif part == 0:
-                        both.append(jnp.where(low, ryz[1, zi, a], ryz[0, zi, a]))
-                    else:
-                        both.append(jnp.where(low, rxyz[part - 1, 1, zi, a], rxyz[part - 1, 0, zi, a]))
-                comb = jnp.where(zleft, both[0], both[1])
-                if part == 0:
-                    pairs = [(4 + x, x) for x in range(16)]
-                elif part == 1:
-                    pairs = [(j, 12 + j) for j in range(4)]
-                else:
-                    pairs = [(20 + j, j) for j in range(4)]
-                for plane, x in pairs:
-                    ext[a, plane, 8 * tile : 8 * tile + 8, 128:256] = roll(comb, -(8 * x + 4), 1)
+                for n in range(4):
+                    value = roll(corner, -(64 * a + 8 * n + 4), 1) if tile == 2 else roll(
+                        edge, -(32 * (2 * a + tile) + 8 * n + 4), 1
+                    )
+                    ext[a, 20 * side + n, 8 * tile : 8 * tile + 8, 128:256] = value
 
 
 def planes_loop(first, last, body):
@@ -223,13 +235,13 @@
 def kernel(
     source, conductance, start, pressure, residual,
     m_fine, m_middle, m_coarse, m_plane, m_tile, m_spread,
-    ek, ea, ev, va, vb, w0, fi0, coef0, diag0, inv0, pyk, pzk, py, pz, pyv, pzv,
+    pwk, pw, pwv, ek, ea, ev, va, vb, w0, fi0, coef0, diag0, inv0, pyk, pzk, py, pz, pyv, pzv,
     ryk, rzk, rxyk, rxzk, ryzk, rxyzk,
     ry, rz, rxy, rxz, ryz, rxyz, ryv, rzv, rxyv, rxzv, ryzv, rxyzv,
-    tk, tf, k1, v1a, v1b, w1, fi1, coef1, diag1, inv1,
+    tk, tkz, zk, tf, tfz, zf, yf, yzf, nr, k1, v1a, v1b, w1, fi1, coef1, diag1, inv1,
     gk, gf, mk, mf, v2a, v2b, w2, coef2, diag2, inv2,
     ck, cf, k3, f3, v3a, v3b, w3, coef3,
-    sem_in, semk_s, semk_r, sem_s, sem_r, semv_s, semv_r, sem1,
+    sem_in, semk_s, semk_r, sem_s, sem_r, semv_s, semv_r, sem1, semn,
 ):
     weights = chebyshev_weights(DEG, SMOOTH_FLOOR)
     coarse_weights = chebyshev_weights(COARSE_ITERS, COARSE_FLOOR)
@@ -239,7 +251,7 @@
     recv_v = (ryv, rzv, rxyv, rxzv, ryzv, rxyzv)
 
     everyone = list(dict.fromkeys(
-        [tuple(s % n for s, n in zip(o, COUNT)) for o in NEAR + PLANE + RING]
+        [tuple(s % n for s, n in zip(o, COUNT)) for o in NEAR + RING + PLANE]
     ))
     barrier = pltpu.get_barrier_semaphore()
     for offset in everyone:
@@ -254,6 +266,192 @@
     ]
     for copy in inputs:
         copy.start()
+
+    def restrict_fine(load, scale):
+        rows = [
+            jnp.concatenate(
+                [load(4 * p) + load(4 * p + 1), load(4 * p + 2) + load(4 * p + 3)], axis=1
+            )
+            for p in range(4)
+        ]
+        mid = dot(jnp.concatenate(rows, axis=0), m_fine[...])
+        wide = jnp.concatenate([mid[16 * p : 16 * p + 16] for p in range(4)], axis=1)
+        left = ones_where(iota((8, 16), 1) // 2 == iota((8, 16), 0))
+        out = dot(left, wide)
+        return [scale * out[:, 128 * p : 128 * p + 128] for p in range(4)]
+
+    lane = iota((8, 128), 1)
+    sub = iota((8, 128), 0)
+    near_z = lane % 64 < 32
+    near_y = sub < 4
+
+    def half_z(first, second, which):
+        if which == 0:
+            return jnp.where(near_z, roll(second, -32, 1), first)
+        return jnp.where(near_z, first, roll(second, 32, 1))
+
+    def half_y(first, second, which):
+        if which == 0:
+            return jnp.where(near_y, roll(second, 4, 0), first)
+        return jnp.where(near_y, first, roll(second, 4, 0))
+
+    def sides(left, right):
+        return (
+            jnp.where(near_z, right, left),
+            jnp.where(near_z, roll(right, -32, 1), roll(left, 32, 1)),
+        )
+
+    def place(put, x, tile, own, side):
+        put(x, tile, jnp.where(lane < 64, own, roll(side, 64, 1)))
+        put(x + 1, tile, jnp.where(lane < 64, roll(own, 64, 1), side))
+
+    def pack_halves(tiles, zpack):
+        for which in range(2):
+            for n in range(2):
+                zpack[which, n] = half_z(tiles[4, 2 * n], tiles[4, 2 * n + 1], which)
+
+    def send_tile(tiles, zpack, ztiles, at):
+        for dx, dy, dz in NEAR:
+            slot = 3 * (1 - dx) + (1 - dy)
+            if dz == 0:
+                send(tiles.at[4], tiles.at[slot], sem1.at[at], sem1.at[at + 1], (dx, dy, dz))
+            else:
+                zi = 0 if dz == 1 else 1
+                send(
+                    zpack.at[zi], ztiles.at[zi, slot], sem1.at[at + 2], sem1.at[at + 3], (dx, dy, dz)
+                )
+
+    def wait_tile(tiles, ztiles, at):
+        wait_bytes(tiles.at[pl.ds(0, 8)], sem1.at[at])
+        wait_bytes(ztiles, sem1.at[at + 2])
+
+    def unpack_tile(tiles, ztiles, put):
+        for i in range(3):
+            for j in range(3):
+                base = 3 * i + j
+                for n in range(2):
+                    both = sides(ztiles[0, base, n], ztiles[1, base, n])
+                    for r in range(2):
+                        q = 2 * n + r
+                        place(put, 8 * i + 2 * q, j, tiles[base, q], both[r])
+
+    def near_slots(kind, xi, yi, zi):
+        if kind == (True, False, False):
+            return 2 * xi, 2
+        if kind == (False, True, False):
+            return 4 + 2 * yi, 2
+        if kind == (False, False, True):
+            return 8 + 2 * zi, 2
+        if kind == (True, True, False):
+            return 12 + 2 * xi + yi, 1
+        if kind == (True, False, True):
+            return 16 + 2 * xi + zi, 1
+        if kind == (False, True, True):
+            return 20 + 2 * yi + zi, 1
+        return 24 + 4 * xi + 2 * yi + zi, 1
+
+    def pack_near():
+        pack_halves(tf, zf)
+        for which in range(2):
+            for n in range(2):
+                yf[which, n] = half_y(tf[4, 2 * n], tf[4, 2 * n + 1], which)
+            for other in range(2):
+                yzf[which, other] = half_z(yf[which, 0], yf[which, 1], other)
+
+    def send_near():
+        for offset in NEAR:
+            dx, dy, dz = offset
+            xi, yi, zi = (0 if d == 1 else 1 for d in offset)
+            kind = (dx != 0, dy != 0, dz != 0)
+            at, size = near_slots(kind, xi, yi, zi)
+            far = 1 - xi
+            if kind == (True, False, False):
+                src = tf.at[4, pl.ds(2 * far, 2)]
+            elif kind == (False, True, False):
+                src = yf.at[yi]
+            elif kind == (False, False, True):
+                src = zf.at[zi]
+            elif kind == (True, True, False):
+                src = yf.at[yi, pl.ds(far, 1)]
+            elif kind == (True, False, True):
+                src = zf.at[zi, pl.ds(far, 1)]
+            else:
+                src = yzf.at[yi, pl.ds(zi, 1)]
+            send(src, nr.at[pl.ds(at, size)], semn.at[0], semn.at[1], offset)
+
+    def unpack_near(put):
+        def get(kind, xi, yi, zi, n=0):
+            return nr[near_slots(kind, xi, yi, zi)[0] + n]
+
+        x_, y_, z_ = (True, False, False), (False, True, False), (False, False, True)
+        xy_, xz_, yz_, all_ = (True, True, False), (True, False, True), (False, True, True), (True,) * 3
+        for n in range(2):
+            both = sides(get(z_, 0, 0, 0, n), get(z_, 0, 0, 1, n))
+            for r in range(2):
+                place(put, 8 + 4 * n + 2 * r, 1, tf[4, 2 * n + r], both[r])
+        for xi in range(2):
+            first = 4 if xi == 0 else 16
+            both = sides(get(xz_, xi, 0, 0), get(xz_, xi, 0, 1))
+            for r in range(2):
+                place(put, first + 2 * r, 1, get(x_, xi, 0, 0, r), both[r])
+        for yi in range(2):
+            tile = 2 * yi
+            both = sides(get(yz_, 0, yi, 0), get(yz_, 0, yi, 1))
+            for n in range(2):
+                own = get(y_, 0, yi, 0, n)
+                place(put, 8 + 4 * n, tile, own, both[n])
+                place(put, 10 + 4 * n, tile, roll(own, 4, 0), roll(both[n], 4, 0))
+            for xi in range(2):
+                first = 4 if xi == 0 else 16
+                side = sides(get(all_, xi, yi, 0), get(all_, xi, yi, 1))[1 - xi]
+                own = get(xy_, xi, yi, 0)
+                place(put, first, tile, own, side)
+                place(put, first + 2, tile, roll(own, 4, 0), roll(side, 4, 0))
+
+    def restrict_middle(rows, scale):
+        i, j = iota((16, 64), 0), iota((16, 64), 1)
+        x = 2 * (i // 8) + (i % 8) // 4
+        left = ones_where((j // 16 == x) & ((j % 8) // 2 == i % 4))
+        mid = dot(left, rows)
+        return scale * dot(jnp.concatenate([mid[0:8], mid[8:16]], axis=1), m_middle[...])
+
+    def send_plane(message, plane, pair):
+        slot = gx * 8 + gy
+        plane[slot] = message[...]
+        for offset in PLANE:
+            send(message, plane.at[slot], sem1.at[pair], sem1.at[pair + 1], offset)
+
+    def restrict_plane(load, scale, message):
+        i, j = iota((8, 32), 0), iota((8, 32), 1)
+        left = ones_where((j // 8 == i // 2) & ((j % 4) // 2 == i % 2))
+        for tile in range(2):
+            wide = jnp.concatenate(
+                [load(ix)[4 * tile : 4 * tile + 4].reshape(32, 128) for ix in range(4)], axis=1
+            )
+            message[tile] = scale * dot(dot(left, wide), m_plane[...])
+
+    def send_ring(message, ring, pair):
+        ring[gz] = message[...]
+        for offset in RING:
+            send(message, ring.at[gz], sem1.at[pair], sem1.at[pair + 1], offset)
+
+    def unpack_ring(ring, out):
+        lane = iota((8, 128), 1)
+        for x in range(8):
+            for tile in range(2):
+                acc = jnp.zeros((8, 128), F32)
+                for z in range(8):
+                    acc = jnp.where(lane // 16 == z, roll(ring[z, tile], 16 * (z - x), 1), acc)
+                out[x, 8 * tile : 8 * tile + 8] = acc
+
+    inputs[0].wait()
+    pack_fine(ek, 1, pyk, pzk, pwk)
+    pl.semaphore_wait(barrier, len(everyone))
+    send_fine(ek, pyk, pzk, pwk, recv_k, semk_s, semk_r)
+    inputs[1].wait()
+    inputs[2].wait()
+    pack_fine(ea, 2, py, pz, pw)
+    send_fine(ea, py, pz, pw, recv, sem_s, sem_r)
 
     i, j = iota((256, 128), 0), iota((256, 128), 1)
     m_fine[...] = ones_where((i // 128 == j // 64) & ((i % 128) // 2 == j % 64), 0.125)
@@ -270,86 +468,14 @@
     i, j = iota((128, 256), 0), iota((128, 256), 1)
     m_tile[...] = ones_where((i // 64 == j // 128) & (i % 64 == (16 + (j % 128) // 2) % 64))
     m_spread[...] = ones_where(i == j // 2)
-
-    def restrict_fine(load, scale):
-        rows = [
-            jnp.concatenate([load(2 * p) + load(2 * p + 1), load(2 * p + 8) + load(2 * p + 9)], axis=1)
-            for p in range(4)
-        ]
-        mid = dot(jnp.concatenate(rows, axis=0), m_fine[...])
-        wide = jnp.concatenate([mid[16 * p : 16 * p + 16] for p in range(4)], axis=1)
-        left = ones_where(iota((8, 16), 1) // 2 == iota((8, 16), 0))
-        out = dot(left, wide)
-        return [scale * out[:, 128 * p : 128 * p + 128] for p in range(4)]
-
-    def send_tile(tiles, pair):
-        for offset in NEAR:
-            slot = 9 * (1 - offset[0]) + 3 * (1 - offset[1]) + (1 - offset[2])
-            send(tiles.at[13], tiles.at[slot], sem1.at[pair], sem1.at[pair + 1], offset)
-
-    def unpack_tile(tiles, put):
-        lane = iota((8, 128), 1)
-        for i in range(3):
-            for j in range(3):
-                base = 9 * i + 3 * j
-                for p in range(4):
-                    own = tiles[base + 1, p]
-                    side = jnp.where(lane % 64 < 32, tiles[base + 2, p], tiles[base, p])
-                    put(8 * i + p, j, jnp.where(lane < 64, own, roll(side, 64, 1)))
-                    put(8 * i + p + 4, j, jnp.where(lane < 64, roll(own, 64, 1), side))
-
-    def restrict_middle(rows, scale):
-        i, j = iota((16, 64), 0), iota((16, 64), 1)
-        x = 2 * (i // 8) + (i % 8) // 4
-        left = ones_where((j // 16 == x) & ((j % 8) // 2 == i % 4))
-        mid = dot(left, rows)
-        return scale * dot(jnp.concatenate([mid[0:8], mid[8:16]], axis=1), m_middle[...])
-
-    def send_plane(message, plane, pair):
-        slot = gx * 8 + gy
-        plane[slot] = message[...]
-        for offset in PLANE:
-            send(message, plane.at[slot], sem1.at[pair], sem1.at[pair + 1], offset)
-
-    def restrict_plane(load, scale, message):
-        i, j = iota((8, 32), 0), iota((8, 32), 1)
-        left = ones_where((j // 8 == i // 2) & ((j % 4) // 2 == i % 2))
-        for tile in range(2):
-            wide = jnp.concatenate(
-                [load(ix)[4 * tile : 4 * tile + 4].reshape(32, 128) for ix in range(4)], axis=1
-            )
-            message[tile] = scale * dot(dot(left, wide), m_plane[...])
-
-    def send_ring(message, ring, pair):
-        ring[gz] = message[...]
-        for offset in RING:
-            send(message, ring.at[gz], sem1.at[pair], sem1.at[pair + 1], offset)
-
-    def unpack_ring(ring, out):
-        lane = iota((8, 128), 1)
-        for x in range(8):
-            for tile in range(2):
-                acc = jnp.zeros((8, 128), F32)
-                for z in range(8):
-                    acc = jnp.where(lane // 16 == z, roll(ring[z, tile], 16 * (z - x), 1), acc)
-                out[x, 8 * tile : 8 * tile + 8] = acc
-
-    inputs[0].wait()
-    pack_fine(ek, 1, pyk, pzk)
     for p, block in enumerate(restrict_fine(lambda x: ek[0, 4 + x, 0:16, 0:128], 0.25)):
-        tk[13, p] = block
-    inputs[1].wait()
-    inputs[2].wait()
-    pack_fine(ea, 2, py, pz)
-    pl.semaphore_wait(barrier, len(everyone))
-    send_fine(ek, pyk, pzk, recv_k, semk_s, semk_r)
-    send_fine(ea, py, pz, recv, sem_s, sem_r)
-
+        tk[4, p] = block
+    pack_halves(tk, zk)
     wait_fine(pyk, recv_k, semk_r)
     unpack_fine(ek, 1, recv_k)
     planes_loop(1, 23, lambda x: make_coefficients(lambda i: ek[0, i], coef0, diag0, inv0, x))
     wait_fine(py, recv, sem_r)
-    send_tile(tk, 0)
+    send_tile(tk, zk, tkz, 0)
     unpack_fine(ea, 2, recv)
 
     def fine_scale(x):
@@ -381,25 +507,26 @@
 
     planes_loop(4, 20, fine_residual)
     for p, block in enumerate(restrict_fine(lambda x: vb[4 + x, 0:16, 0:128], 1.0)):
-        tf[13, p] = block
-    send_tile(tf, 2)
-
-    wait_bytes(tk.at[pl.ds(0, 26)], sem1.at[1])
+        tf[4, p] = block
+    pack_near()
+    send_near()
+
+    wait_tile(tk, tkz, 1)
 
     def put_k1(x, tile, value):
         k1[x, 8 * tile : 8 * tile + 8] = value
 
-    unpack_tile(tk, put_k1)
+    unpack_tile(tk, tkz, put_k1)
     mk[...] = restrict_middle(k1[8:16, 8:16].reshape(64, 128), 0.25)
-    send_plane(mk, gk, 4)
+    send_plane(mk, gk, 8)
     planes_loop(1, 23, lambda x: make_coefficients(lambda i: k1[i], coef1, diag1, inv1, x))
 
-    wait_bytes(tf.at[pl.ds(0, 26)], sem1.at[3])
+    wait_bytes(nr, semn.at[1])
 
     def put_f1(x, tile, value):
         fi1[x, 8 * tile : 8 * tile + 8] = value
 
-    unpack_tile(tf, put_f1)
+    unpack_near(put_f1)
 
     def middle_first(x):
         scaled = fi1[x] * inv1[x]
@@ -408,8 +535,6 @@
         w1[x] = change
         v1a[x] = change
 
-    planes_loop(1, 23, middle_first)
-
     def middle_sweep(load, out, index, first, last):
         carry, weight = weights[index]
 
@@ -421,8 +546,12 @@
 
         planes_loop(first, last, body)
 
-    middle_sweep(lambda i: v1a[i], v1b, 1, 2, 22)
-    middle_sweep(lambda i: v1b[i], v1a, 2, 3, 21)
+    def middle_before(first, last):
+        planes_loop(first, last, middle_first)
+        middle_sweep(lambda i: v1a[i], v1b, 1, first + 1, last - 1)
+        middle_sweep(lambda i: v1b[i], v1a, 2, first + 2, last - 2)
+
+    middle_before(5, 19)
 
     def middle_residual(x):
         _, r = scaled_residual(lambda i: v1a[i], coef1, fi1, x)
@@ -430,15 +559,14 @@
 
     planes_loop(8, 16, middle_residual)
     mf[...] = restrict_middle(v1b[8:16, 8:16].reshape(64, 128), 1.0)
-    send_plane(mf, gf, 6)
-    pack_fine(ev, 1, pyv, pzv)
-    send_fine(ev, pyv, pzv, recv_v, semv_s, semv_r)
-
-    wait_bytes(gk.at[pl.ds(0, 31)], sem1.at[5])
+    send_plane(mf, gf, 12)
+    send_tile(tf, zf, tfz, 4)
+
+    wait_bytes(gk.at[pl.ds(0, 31)], sem1.at[9])
     k2 = gk.reshape(4, 8, 8, 128)
     f2 = gf.reshape(4, 8, 8, 128)
     restrict_plane(lambda ix: k2[ix], 0.25, ck.at[8])
-    send_ring(ck.at[8], ck, 8)
+    send_ring(ck.at[8], ck, 10)
     for ix in range(4):
         k, around = shifts_plane(k2, ix)
         faces = [0.5 * (k + other) for other in around]
@@ -449,7 +577,7 @@
         diag2[ix] = d
         inv2[ix] = inv
 
-    wait_bytes(gf.at[pl.ds(0, 31)], sem1.at[7])
+    wait_bytes(gf.at[pl.ds(0, 31)], sem1.at[13])
     for ix in range(4):
         change = weights[0][1] * (f2[ix] * inv2[ix])
         w2[ix] = change
@@ -475,9 +603,15 @@
     for ix in range(4):
         v2b[ix] = plane_residual(v2a, ix)[1] * diag2[ix]
     restrict_plane(lambda ix: v2b[ix], 1.0, cf.at[8])
-    send_ring(cf.at[8], cf, 10)
-
-    wait_bytes(ck.at[pl.ds(0, 7)], sem1.at[9])
+    send_ring(cf.at[8], cf, 14)
+
+    pack_fine(ev, 1, pyv, pzv, pwv)
+    send_fine(ev, pyv, pzv, pwv, recv_v, semv_s, semv_r)
+    wait_tile(tf, tfz, 5)
+    unpack_tile(tf, tfz, put_f1)
+    middle_before(1, 23)
+
+    wait_bytes(ck.at[pl.ds(0, 7)], sem1.at[11])
     unpack_ring(ck, k3)
     for x in range(8):
         k = k3[x]
@@ -488,7 +622,7 @@
         for n in range(6):
             coef3[n, x] = faces[n] * inv
         coef3[6, x] = inv
-    wait_bytes(cf.at[pl.ds(0, 7)], sem1.at[11])
+    wait_bytes(cf.at[pl.ds(0, 7)], sem1.at[15])
     unpack_ring(cf, f3)
     for x in range(8):
         scaled = f3[x] * coef3[6, x]
@@ -572,12 +706,13 @@
     wait_fine(pyk, recv_k, semk_s)
     wait_fine(py, recv, sem_s)
     wait_fine(pyv, recv_v, semv_s)
-    wait_bytes(tk.at[pl.ds(0, 26)], sem1.at[0])
-    wait_bytes(tf.at[pl.ds(0, 26)], sem1.at[2])
-    wait_bytes(gk.at[pl.ds(0, 31)], sem1.at[4])
-    wait_bytes(gf.at[pl.ds(0, 31)], sem1.at[6])
-    wait_bytes(ck.at[pl.ds(0, 7)], sem1.at[8])
-    wait_bytes(cf.at[pl.ds(0, 7)], sem1.at[10])
+    wait_tile(tk, tkz, 0)
+    wait_bytes(nr, semn.at[0])
+    wait_tile(tf, tfz, 4)
+    wait_bytes(gk.at[pl.ds(0, 31)], sem1.at[8])
+    wait_bytes(ck.at[pl.ds(0, 7)], sem1.at[10])
+    wait_bytes(gf.at[pl.ds(0, 31)], sem1.at[12])
+    wait_bytes(cf.at[pl.ds(0, 7)], sem1.at[14])
 
 
 def vmem(*shape):
@@ -587,7 +722,7 @@
 def fine_buffers(count):
     return [
         vmem(2, count, 8, 8, 128), vmem(2, count, 2, 8, 128), vmem(2, 2, count, 2, 8, 128),
-        vmem(2, 2, count, 2, 8, 128), vmem(2, 2, count, 8, 128), vmem(2, 2, 2, count, 8, 128),
+        vmem(2, 2, 8, 128), vmem(2, 2, count, 8, 128), vmem(2, 2, 2, 8, 128),
     ]
 
 
@@ -598,13 +733,16 @@
     coarse = (8, 16, 128)
     scratch = [
         vmem(256, 128), vmem(256, 128), vmem(256, 128), vmem(512, 128), vmem(128, 256), vmem(128, 256),
+        vmem(2, 8, 128), vmem(2, 8, 128), vmem(2, 8, 128),
         vmem(1, *fine), vmem(2, *fine), vmem(1, *fine), vmem(*fine), vmem(*fine), vmem(*fine), vmem(*fine),
         vmem(6, *fine), vmem(*fine), vmem(*fine),
         vmem(2, 1, 8, 8, 128), vmem(1, 2, 8, 128), vmem(2, 2, 8, 8, 128), vmem(2, 2, 8, 128), vmem(2, 1, 8, 8, 128), vmem(1, 2, 8, 128),
     ]
     scratch += fine_buffers(1) + fine_buffers(2) + fine_buffers(1)
     scratch += [
-        vmem(27, 4, 8, 128), vmem(27, 4, 8, 128), vmem(*middle), vmem(*middle), vmem(*middle),
+        vmem(9, 4, 8, 128), vmem(2, 9, 2, 8, 128), vmem(2, 2, 8, 128),
+        vmem(9, 4, 8, 128), vmem(2, 9, 2, 8, 128), vmem(2, 2, 8, 128),
+        vmem(2, 2, 8, 128), vmem(2, 2, 8, 128), vmem(32, 8, 128), vmem(*middle), vmem(*middle), vmem(*middle),
         vmem(*middle), vmem(*middle), vmem(6, *middle), vmem(*middle), vmem(*middle),
         vmem(32, 8, 128), vmem(32, 8, 128), vmem(8, 128), vmem(8, 128),
         vmem(*plane), vmem(*plane), vmem(*plane), vmem(6, *plane), vmem(*plane), vmem(*plane),
@@ -614,7 +752,7 @@
         pltpu.SemaphoreType.DMA((7,)), pltpu.SemaphoreType.DMA((7,)),
         pltpu.SemaphoreType.DMA((7,)), pltpu.SemaphoreType.DMA((7,)),
         pltpu.SemaphoreType.DMA((7,)), pltpu.SemaphoreType.DMA((7,)),
-        pltpu.SemaphoreType.DMA((12,)),
+        pltpu.SemaphoreType.DMA((16,)), pltpu.SemaphoreType.DMA((2,)),
     ]
     block = jax.ShapeDtypeStruct(source.shape, F32)
     whole = pl.BlockSpec(memory_space=pltpu.VMEM)

time: 49.2 us -> 46.2 us (0.939)
  Pallas kernels: 44.4 us -> 41.4 us
    pallas_call x1, Pallas kernels: 44.4 us -> 41.4 us  [per_device(): pl.pallas_call(kernel, out_shape=(block, block), in_specs=[pl.BlockSpec(m...]
where the time goes in v3:
time: 46.2 us; the launch traced here: 46.1 us
  Pallas kernels  41.4 us (90%)
  local copies, waits for them, and re-layouts  4.02 us (9%)
  between operations  0.65 us (1%)
    pallas_call x1, Pallas kernels, per_device(): pl.pallas_call(kernel, out_shape=(block, block), in_specs=[pl.BlockSpec(m...  41.4 us
    unnamed x8, local copies, waits for them, and re-layouts  4.02 us

profile of v3, /device:TPU:1, one launch (start us, length us, event | category | flops | bytes accessed | tf_op | source)
XLA Modules:
  0.0 46.1 jit_solution(3386566761445487347)
XLA Ops:
  0.6 0.0 copy-start
  0.6 0.9 %copy-done = f32[16,16,128]{2,1,0:T(8,128)S(1)} copy-done((f32[16,16,128]{2,1,0:T(8,128)S(1)}, f32[16,16,128]{2,1,0:T(8,128)}, u32[]{:S(2)}) %copy-start) | copy-done | bytes 131096
  1.5 0.0 copy-start.1
  1.5 0.9 %copy-done.1 = f32[16,16,128]{2,1,0:T(8,128)S(1)} copy-done((f32[16,16,128]{2,1,0:T(8,128)S(1)}, f32[16,16,128]{2,1,0:T(8,128)}, u32[]{:S(2)}) %copy-start.1) | copy-done | bytes 131096
  2.4 0.0 copy-start.2
  2.4 0.9 %copy-done.2 = f32[16,16,128]{2,1,0:T(8,128)S(1)} copy-done((f32[16,16,128]{2,1,0:T(8,128)S(1)}, f32[16,16,128]{2,1,0:T(8,128)}, u32[]{:S(2)}) %copy-start.2) | copy-done | bytes 131096
  3.3 41.4 %shard_map.50 = (f32[16,16,128]{2,1,0:T(8,128)S(1)}, f32[16,16,128]{2,1,0:T(8,128)S(1)}) custom-call(f32[16,16,128]{2,1,0:T(8,128)S(1)} %copy-done, f32[16,16,128]{2,1,0:T(8,128)S(1)} %copy-done.1, f32[16,16,128]{2,1,0:T(8,128)S(1)} %copy-done.2), custom_call_target="tpu_custom_call" | custom-call | tf_op jit(solution)/shard_map/pallas_call | solution.py:759
  44.8 0.7 %copy.7 = f32[16,16,128]{2,1,0:T(8,128)} copy(f32[16,16,128]{2,1,0:T(8,128)S(1)} %get-tuple-element.4) | data formatting | bytes 262144
  45.4 0.7 %copy.8 = f32[16,16,128]{2,1,0:T(8,128)} copy(f32[16,16,128]{2,1,0:T(8,128)S(1)} %get-tuple-element.5) | data formatting | bytes 262144
Async XLA Ops:
  0.6 0.9 %copy-start = (f32[16,16,128]{2,1,0:T(8,128)S(1)}, f32[16,16,128]{2,1,0:T(8,128)}, u32[]{:S(2)}) copy-start(f32[16,16,128]{2,1,0:T(8,128)} %source.1) | copy-start | bytes 393220
  1.5 0.9 %copy-start.1 = (f32[16,16,128]{2,1,0:T(8,128)S(1)}, f32[16,16,128]{2,1,0:T(8,128)}, u32[]{:S(2)}) copy-start(f32[16,16,128]{2,1,0:T(8,128)} %conductance.1) | copy-start | bytes 393220
  2.4 0.9 %copy-start.2 = (f32[16,16,128]{2,1,0:T(8,128)S(1)}, f32[16,16,128]{2,1,0:T(8,128)}, u32[]{:S(2)}) copy-start(f32[16,16,128]{2,1,0:T(8,128)} %start.1) | copy-start | bytes 393220

commit v4 on v3

--- a/solution.py
+++ b/solution.py
@@ -60,8 +60,23 @@
     return pltpu.roll(value, shift % size, dim)
 
 
-def dot(left, right):
-    return jnp.dot(left, right, precision=lax.Precision.HIGHEST, preferred_element_type=F32)
+def parts_of(value):
+    first = value.astype(jnp.bfloat16).astype(F32)
+    rest = value - first
+    second = rest.astype(jnp.bfloat16).astype(F32)
+    return first, second, rest - second
+
+
+def dot(value, matrix):
+    rows = value.shape[0]
+    out = jnp.dot(jnp.concatenate(parts_of(value), axis=0), matrix, preferred_element_type=F32)
+    return (out[2 * rows :] + out[rows : 2 * rows]) + out[:rows]
+
+
+def dot_rows(matrix, value):
+    columns = value.shape[1]
+    out = jnp.dot(matrix, jnp.concatenate(parts_of(value), axis=1), preferred_element_type=F32)
+    return (out[:, 2 * columns :] + out[:, columns : 2 * columns]) + out[:, :columns]
 
 
 def ones_where(mask, scale=1.0):
@@ -277,7 +292,7 @@
         mid = dot(jnp.concatenate(rows, axis=0), m_fine[...])
         wide = jnp.concatenate([mid[16 * p : 16 * p + 16] for p in range(4)], axis=1)
         left = ones_where(iota((8, 16), 1) // 2 == iota((8, 16), 0))
-        out = dot(left, wide)
+        out = dot_rows(left, wide)
         return [scale * out[:, 128 * p : 128 * p + 128] for p in range(4)]
 
     lane = iota((8, 128), 1)
@@ -412,7 +427,7 @@
         i, j = iota((16, 64), 0), iota((16, 64), 1)
         x = 2 * (i // 8) + (i % 8) // 4
         left = ones_where((j // 16 == x) & ((j % 8) // 2 == i % 4))
-        mid = dot(left, rows)
+        mid = dot_rows(left, rows)
         return scale * dot(jnp.concatenate([mid[0:8], mid[8:16]], axis=1), m_middle[...])
 
     def send_plane(message, plane, pair):
@@ -428,7 +443,7 @@
             wide = jnp.concatenate(
                 [load(ix)[4 * tile : 4 * tile + 4].reshape(32, 128) for ix in range(4)], axis=1
             )
-            message[tile] = scale * dot(dot(left, wide), m_plane[...])
+            message[tile] = scale * dot(dot_rows(left, wide), m_plane[...])
 
     def send_ring(message, ring, pair):
         ring[gz] = message[...]
@@ -474,8 +489,8 @@
     wait_fine(pyk, recv_k, semk_r)
     unpack_fine(ek, 1, recv_k)
     planes_loop(1, 23, lambda x: make_coefficients(lambda i: ek[0, i], coef0, diag0, inv0, x))
+    send_tile(tk, zk, tkz, 0)
     wait_fine(py, recv, sem_r)
-    send_tile(tk, zk, tkz, 0)
     unpack_fine(ea, 2, recv)
 
     def fine_scale(x):
@@ -483,16 +498,22 @@
 
     planes_loop(1, 23, fine_scale)
 
-    def fine_sweep(load, out, index, first, last, extra=None):
+    def fine_sweep(load, out, index, first, last):
         carry, weight = weights[index]
 
         def body(x):
             v, r = scaled_residual(load, coef0, fi0, x)
             change = weight * r if index == 0 else carry * w0[x] + weight * r
-            w0[x] = change
-            out[x] = v + change
-            if extra is not None:
-                extra(x, v + change)
+            reach = 3 - index - max(4 - x, x - 19, 0)
+            cuts = [(slice(0, 16), slice(0, 128))]
+            if reach > 0:
+                cuts += [(slice(16, 24), slice(0, 128)), (slice(0, 16), slice(128, 256))]
+            if reach > 1:
+                cuts += [(slice(16, 24), slice(128, 256))]
+            for cut in cuts:
+                if index < 2:
+                    w0[(x,) + cut] = change[cut]
+                out[(x,) + cut] = (v + change)[cut]
 
         planes_loop(first, last, body)
 
@@ -652,7 +673,7 @@
     wide = jnp.concatenate([mid[16 * ix : 16 * ix + 16] for ix in range(4)], axis=1)
     i, j = iota((64, 16), 0), iota((64, 16), 1)
     left = ones_where(j == 2 * (i // 8) + (i % 4) // 2)
-    spread = dot(left, wide)
+    spread = dot_rows(left, wide)
     for ix in range(4):
         v2b[ix] = v2a[ix] + spread[:, 128 * ix : 128 * ix + 128].reshape(8, 8, 128)
     plane_sweep(v2b, v2a, 0)
@@ -666,7 +687,7 @@
     wide = jnp.concatenate([mid[8 * t : 8 * t + 8] for t in range(9)], axis=1)
     i, j = iota((32, 8), 0), iota((32, 8), 1)
     left = ones_where(j == (i // 16) * 4 + (i % 8) // 2)
-    spread = dot(left, wide)
+    spread = dot_rows(left, wide)
     for t in range(9):
         for h in range(2):
             for x in range(4):
@@ -685,7 +706,7 @@
     wide = jnp.concatenate([v1a[6 + p] for p in range(12)], axis=1)
     i, j = iota((24, 24), 0), iota((24, 24), 1)
     left = ones_where(j == jnp.where(i < 20, 8 + i // 2, i // 2 - 4))
-    mid = dot(left, wide)
+    mid = dot_rows(left, wide)
     spread = dot(
         jnp.concatenate([mid[:, 128 * p : 128 * p + 128] for p in range(12)], axis=0), m_spread[...]
     )

time: 46.2 us -> 45.5 us (0.985)
  Pallas kernels: 41.4 us -> 40.7 us
    pallas_call x1, Pallas kernels: 41.4 us -> 40.7 us  [per_device(): pl.pallas_call(kernel, out_shape=(block, block), in_specs=[pl.BlockSpec(m...]
where the time goes in v4:
time: 45.5 us; the launch traced here: 45.3 us
  Pallas kernels  40.7 us (89%)
  local copies, waits for them, and re-layouts  4.02 us (9%)
  between operations  0.65 us (1%)
    pallas_call x1, Pallas kernels, per_device(): pl.pallas_call(kernel, out_shape=(block, block), in_specs=[pl.BlockSpec(m...  40.7 us
    unnamed x8, local copies, waits for them, and re-layouts  4.02 us

profile of v4, /device:TPU:1, one launch (start us, length us, event | category | flops | bytes accessed | tf_op | source)
XLA Modules:
  0.0 45.3 jit_solution(56468723105627409)
XLA Ops:
  0.6 0.0 copy-start
  0.6 0.9 %copy-done = f32[16,16,128]{2,1,0:T(8,128)S(1)} copy-done((f32[16,16,128]{2,1,0:T(8,128)S(1)}, f32[16,16,128]{2,1,0:T(8,128)}, u32[]{:S(2)}) %copy-start) | copy-done | bytes 131096
  1.5 0.0 copy-start.1
  1.5 0.9 %copy-done.1 = f32[16,16,128]{2,1,0:T(8,128)S(1)} copy-done((f32[16,16,128]{2,1,0:T(8,128)S(1)}, f32[16,16,128]{2,1,0:T(8,128)}, u32[]{:S(2)}) %copy-start.1) | copy-done | bytes 131096
  2.4 0.0 copy-start.2
  2.4 0.9 %copy-done.2 = f32[16,16,128]{2,1,0:T(8,128)S(1)} copy-done((f32[16,16,128]{2,1,0:T(8,128)S(1)}, f32[16,16,128]{2,1,0:T(8,128)}, u32[]{:S(2)}) %copy-start.2) | copy-done | bytes 131096
  3.3 40.7 %shard_map.50 = (f32[16,16,128]{2,1,0:T(8,128)S(1)}, f32[16,16,128]{2,1,0:T(8,128)S(1)}) custom-call(f32[16,16,128]{2,1,0:T(8,128)S(1)} %copy-done, f32[16,16,128]{2,1,0:T(8,128)S(1)} %copy-done.1, f32[16,16,128]{2,1,0:T(8,128)S(1)} %copy-done.2), custom_call_target="tpu_custom_call" | custom-call | tf_op jit(solution)/shard_map/pallas_call | solution.py:780
  44.0 0.7 %copy.7 = f32[16,16,128]{2,1,0:T(8,128)} copy(f32[16,16,128]{2,1,0:T(8,128)S(1)} %get-tuple-element.4) | data formatting | bytes 262144
  44.7 0.7 %copy.8 = f32[16,16,128]{2,1,0:T(8,128)} copy(f32[16,16,128]{2,1,0:T(8,128)S(1)} %get-tuple-element.5) | data formatting | bytes 262144
Async XLA Ops:
  0.6 0.9 %copy-start = (f32[16,16,128]{2,1,0:T(8,128)S(1)}, f32[16,16,128]{2,1,0:T(8,128)}, u32[]{:S(2)}) copy-start(f32[16,16,128]{2,1,0:T(8,128)} %source.1) | copy-start | bytes 393220
  1.5 0.9 %copy-start.1 = (f32[16,16,128]{2,1,0:T(8,128)S(1)}, f32[16,16,128]{2,1,0:T(8,128)}, u32[]{:S(2)}) copy-start(f32[16,16,128]{2,1,0:T(8,128)} %conductance.1) | copy-start | bytes 393220
  2.4 0.9 %copy-start.2 = (f32[16,16,128]{2,1,0:T(8,128)S(1)}, f32[16,16,128]{2,1,0:T(8,128)}, u32[]{:S(2)}) copy-start(f32[16,16,128]{2,1,0:T(8,128)} %start.1) | copy-start | bytes 393220

commit v5 on v4

--- a/solution.py
+++ b/solution.py
@@ -30,6 +30,14 @@
 PLANE = [(a, b, 0) for a in range(4) for b in range(8) if (a, b) != (0, 0)]
 RING = [(0, 0, c) for c in range(1, 8)]
 
+
+def hops(offset):
+    x, y, z = (min(s % n, n - s % n) for s, n in zip(offset, COUNT))
+    return x + (y + 1) // 2 + z
+
+
+PLANE.sort(key=lambda o: -hops(o))
+RING.sort(key=lambda o: -hops(o))
 
 def chebyshev_weights(number, floor_value):
     centre = 0.5 * (UPPER_BOUND + floor_value)

time: 45.5 us -> 44.8 us (0.985)
  Pallas kernels: 40.7 us -> 40 us
    pallas_call x1, Pallas kernels: 40.7 us -> 40 us  [per_device(): pl.pallas_call(kernel, out_shape=(block, block), in_specs=[pl.BlockSpec(m...]
where the time goes in v5:
time: 44.8 us; the launch traced here: 44.7 us
  Pallas kernels  40 us (89%)
  local copies, waits for them, and re-layouts  4.02 us (9%)
  between operations  0.65 us (1%)
    pallas_call x1, Pallas kernels, per_device(): pl.pallas_call(kernel, out_shape=(block, block), in_specs=[pl.BlockSpec(m...  40 us
    unnamed x8, local copies, waits for them, and re-layouts  4.02 us

profile of v5, /device:TPU:1, one launch (start us, length us, event | category | flops | bytes accessed | tf_op | source)
XLA Modules:
  0.0 44.7 jit_solution(15667136528457293415)
XLA Ops:
  0.6 0.0 copy-start
  0.6 0.9 %copy-done = f32[16,16,128]{2,1,0:T(8,128)S(1)} copy-done((f32[16,16,128]{2,1,0:T(8,128)S(1)}, f32[16,16,128]{2,1,0:T(8,128)}, u32[]{:S(2)}) %copy-start) | copy-done | bytes 131096
  1.5 0.0 copy-start.1
  1.5 0.9 %copy-done.1 = f32[16,16,128]{2,1,0:T(8,128)S(1)} copy-done((f32[16,16,128]{2,1,0:T(8,128)S(1)}, f32[16,16,128]{2,1,0:T(8,128)}, u32[]{:S(2)}) %copy-start.1) | copy-done | bytes 131096
  2.4 0.0 copy-start.2
  2.4 0.9 %copy-done.2 = f32[16,16,128]{2,1,0:T(8,128)S(1)} copy-done((f32[16,16,128]{2,1,0:T(8,128)S(1)}, f32[16,16,128]{2,1,0:T(8,128)}, u32[]{:S(2)}) %copy-start.2) | copy-done | bytes 131096
  3.3 40.0 %shard_map.50 = (f32[16,16,128]{2,1,0:T(8,128)S(1)}, f32[16,16,128]{2,1,0:T(8,128)S(1)}) custom-call(f32[16,16,128]{2,1,0:T(8,128)S(1)} %copy-done, f32[16,16,128]{2,1,0:T(8,128)S(1)} %copy-done.1, f32[16,16,128]{2,1,0:T(8,128)S(1)} %copy-done.2), custom_call_target="tpu_custom_call" | custom-call | tf_op jit(solution)/shard_map/pallas_call | solution.py:788
  43.4 0.7 %copy.7 = f32[16,16,128]{2,1,0:T(8,128)} copy(f32[16,16,128]{2,1,0:T(8,128)S(1)} %get-tuple-element.4) | data formatting | bytes 262144
  44.0 0.7 %copy.8 = f32[16,16,128]{2,1,0:T(8,128)} copy(f32[16,16,128]{2,1,0:T(8,128)S(1)} %get-tuple-element.5) | data formatting | bytes 262144
Async XLA Ops:
  0.6 0.9 %copy-start = (f32[16,16,128]{2,1,0:T(8,128)S(1)}, f32[16,16,128]{2,1,0:T(8,128)}, u32[]{:S(2)}) copy-start(f32[16,16,128]{2,1,0:T(8,128)} %source.1) | copy-start | bytes 393220
  1.5 0.9 %copy-start.1 = (f32[16,16,128]{2,1,0:T(8,128)S(1)}, f32[16,16,128]{2,1,0:T(8,128)}, u32[]{:S(2)}) copy-start(f32[16,16,128]{2,1,0:T(8,128)} %conductance.1) | copy-start | bytes 393220
  2.4 0.9 %copy-start.2 = (f32[16,16,128]{2,1,0:T(8,128)S(1)}, f32[16,16,128]{2,1,0:T(8,128)}, u32[]{:S(2)}) copy-start(f32[16,16,128]{2,1,0:T(8,128)} %start.1) | copy-start | bytes 393220
